TPU v7x, 32 devices: a whole 2x2x4 slice. The times are simulated.
32 devices in a mesh: gx: 8 (over y, x, core), gy: 4 (over z).
Axes of the slice: x: 2, y: 2, z: 4, core: 2. Of those that a mesh axis runs over, the one named last changes fastest.
Arguments:
- displacement: float32 [3, 16, 8, 128], P(None, 'gx', 'gy'), may hold values from -0.3 to 0.3
- velocity: float32 [3, 16, 8, 128], P(None, 'gx', 'gy'), may hold values from -30 to 30
- forces: float32 [3, 16, 8, 128], P(None, 'gx', 'gy'), may hold values from -30 to 30
- heights: int32 [16, 8, 128], P('gx', 'gy'), may hold values from 0 to 127, as said below
- counts: int32 [16, 8], P('gx', 'gy'), may hold values from 64 to 128
- neighbours: int32 [8, 16, 8, 128], P(None, 'gx', 'gy'), may hold values from 0 to 1151, as said below
- plan: int32 [8, 4, 4, 1], P('gx', 'gy'), may hold values from 0 to 3; in each aligned block of 4 rows (0 to 3, 4 to 7, ..., all dimensions but the last counted through in order) at most 2 rows name the same one
Outputs:
- arrived: float32 [8, 4, 4, 2, 7, 128], P('gx', 'gy')
Inputs may be any that keep to these rules, and one draw needn't show every extreme that they name: `heights`: each cell column's 128 entries name every layer from 0 to 127 once. `neighbours`: entry c * 128 + s names slot s of the column at offset (c // 3 - 1, c % 3 - 1) in x and y; a slot never names itself. `plan`: among one device's 2 * 2 cell columns at most 2 name the same new owner.
All inputs are finite; a program needn't handle non-finite values.
Results may differ from a plain program's by a relative error of at most 0.0003.
Values sent between devices are 32-bit elements; how exact they have to be, the bound alone decides.
No kernel may reach another device: no remote copies, remote signals or barrier semaphores. Data moves between devices by JAX's collectives and lax.ppermute only.
A program may use at most 64 MiB of HBM per device.

v0:
```python
import jax
import jax.numpy as jnp
from jax import lax
from jax.sharding import PartitionSpec as P

repulse_a = 1830.8
attract_b = 471.18
decay_one = 2.4799
decay_two = 1.7322
beta_t = 1.1e-06
expo_n = 0.78734
coeff_c2 = 100390.0**2
coeff_d2 = 16.217**2
coeff_h = -0.59825
spacing = 2.4
time_step = 0.001
half_step = 0.0005
force_scale = 9648.53 / 28.0855


def shifted(value, axis, steps):
    count = lax.axis_size(axis)
    first, last = (max(0, -steps), min(count, count - steps))
    return lax.ppermute(value, axis, [(source, source + steps) for source in range(first, last)])


def extended(array, sides, width):
    for axis, dim in sides:
        size, length = (lax.axis_size(axis), array.shape[dim])
        up = [(i, (i + 1) % size) for i in range(size - 1)]
        down = [(j, i) for i, j in up]
        last = lax.slice_in_dim(array, length - width, length, axis=dim)
        first = lax.slice_in_dim(array, 0, width, axis=dim)
        before = lax.ppermute(last, axis, up)
        after = lax.ppermute(first, axis, down)
        array = jnp.concatenate([before, array, after], axis=dim)
    return array


def cutoff(radius):
    smooth = 0.5 - 0.5 * jnp.sin(0.5 * jnp.pi * (radius - 2.85) / 0.15)
    return jnp.where(radius < 2.7, 1.0, jnp.where(radius > 3.0, 0.0, smooth))


def cell_energy(center, nearby):
    offsets = nearby[:3] - center[:3][:, :, :, None, :]
    radius = jnp.sqrt(jnp.maximum(jnp.sum(offsets * offsets, axis=0), 1.0))
    weight = cutoff(radius) * nearby[3]
    direction = offsets / radius
    cosine = direction[0][:, :, :, None, :] * direction[0][:, :, None, :, :]
    cosine = cosine + direction[1][:, :, :, None, :] * direction[1][:, :, None, :, :]
    cosine = cosine + direction[2][:, :, :, None, :] * direction[2][:, :, None, :, :]
    spread = (coeff_h - cosine) ** 2
    angular = 1.0 + coeff_c2 * spread / (coeff_d2 * (coeff_d2 + spread))
    others = 1.0 - jnp.eye(nearby.shape[3], dtype=cosine.dtype)[:, :, None]
    bond_sum = jnp.maximum(jnp.sum(angular * weight[:, :, None, :, :] * others, axis=3), 1.0)
    bond_order = (1.0 + jnp.exp(expo_n * jnp.log(beta_t * bond_sum))) ** (-0.5 / expo_n)
    pair_terms = weight * (
        repulse_a * jnp.exp(-decay_one * radius)
        - attract_b * jnp.exp(-decay_two * radius) * bond_order
    )
    return 0.5 * center[3] * jnp.sum(pair_terms, axis=2)


def flat_index(neighbours):
    width_x, width_y = (neighbours.shape[1], neighbours.shape[2])
    return jnp.transpose(neighbours, (1, 2, 0, 3)).reshape(width_x, width_y, -1)


def gather_nearby(points, gather_index):
    width_x, width_y = (gather_index.shape[0], gather_index.shape[1])
    slots = points.shape[3]
    pieces = [
        points[:, 1 + shift_x : 1 + shift_x + width_x, 1 + shift_y : 1 + shift_y + width_y]
        for shift_x in (-1, 0, 1)
        for shift_y in (-1, 0, 1)
    ]
    joined = jnp.concatenate(pieces, axis=3)
    wide_index = jnp.broadcast_to(gather_index[None], (4,) + gather_index.shape)
    picked = jnp.take_along_axis(joined, wide_index, axis=3)
    return picked.reshape(4, width_x, width_y, gather_index.shape[2] // slots, slots)


def tersoff_total(coords, occupied, gather_index):
    points = jnp.concatenate([coords, occupied], axis=0)
    center = points[:, 1:-1, 1:-1]
    return jnp.sum(cell_energy(center, gather_nearby(points, gather_index)))


def return_y(strip, offset):
    return shifted(strip, "gy", offset)


def return_x(strip, offset):
    return shifted(strip, "gx", offset)


def forces_returned(state, gather_index):
    padded = extended(state, (("gx", 1), ("gy", 2)), 1)
    grads = jax.grad(tersoff_total)(padded[:3], padded[3:], gather_index)
    width_y = grads.shape[2] - 2
    from_above = return_y(grads[:, :, 0], -1)
    from_below = return_y(grads[:, :, width_y + 1], 1)
    grads = grads.at[:, :, width_y].add(from_above).at[:, :, 1].add(from_below)[:, :, 1:-1]
    width_x = grads.shape[1] - 2
    from_right = return_x(grads[:, 0], -1)
    from_left = return_x(grads[:, width_x + 1], 1)
    grads = grads.at[:, width_x].add(from_right).at[:, 1].add(from_left)[:, 1:-1]
    return -grads


def pack_columns(rows, plan_rows, groups, capacity):
    target = plan_rows[:, 0]
    chosen = (target[:, None] == jnp.arange(groups, dtype=jnp.int32)[None, :]).astype(jnp.int32)
    earlier = jnp.cumsum(chosen, axis=0) - chosen
    place = target * capacity + jnp.sum(chosen * earlier, axis=1)
    dispatch = (jnp.arange(groups * capacity, dtype=jnp.int32)[:, None] == place[None, :]).astype(
        rows.dtype
    )
    packed = jnp.einsum("rc,acs->ras", dispatch, rows, precision=lax.Precision.HIGHEST)
    return packed.reshape(groups, capacity, rows.shape[0], rows.shape[2])


def per_device(displacement, velocity, forces, heights, counts, neighbours, plan):
    cells_x, cells_y, slots = heights.shape
    first_x = lax.axis_index("gx") * cells_x
    first_y = lax.axis_index("gy") * cells_y
    along_x = ((first_x + jnp.arange(cells_x, dtype=jnp.int32)).astype(jnp.float32) + 0.5) * spacing
    along_y = ((first_y + jnp.arange(cells_y, dtype=jnp.int32)).astype(jnp.float32) + 0.5) * spacing
    along_z = (heights.astype(jnp.float32) + 0.5) * spacing
    lattice = jnp.stack(
        [
            jnp.broadcast_to(along_x[:, None, None], along_z.shape),
            jnp.broadcast_to(along_y[None, :, None], along_z.shape),
            along_z,
        ]
    )
    occupied = (heights < counts[:, :, None]).astype(jnp.float32)
    gather_index = flat_index(neighbours)
    offset, speed, force_now = (displacement, velocity, forces)
    speed = speed + half_step * (force_now * force_scale)
    offset = offset + time_step * speed
    state = jnp.concatenate([lattice + offset, occupied[None]], axis=0)
    force_now = forces_returned(state, gather_index)
    speed = speed + half_step * (force_now * force_scale)
    columns = cells_x * cells_y
    groups = lax.axis_size("gy")
    capacity = max(2, (2 * columns + groups - 1) // groups)
    rows = jnp.concatenate([offset, speed, occupied[None]], axis=0).reshape(7, columns, slots)
    packed = pack_columns(rows, plan[0, 0], groups, capacity)
    arrived = lax.all_to_all(packed, "gy", split_axis=0, concat_axis=0, tiled=True)
    return arrived[None, None]


def solution(mesh):
    in_specs = (
        P(None, "gx", "gy", None),
        P(None, "gx", "gy", None),
        P(None, "gx", "gy", None),
        P("gx", "gy", None),
        P("gx", "gy"),
        P(None, "gx", "gy", None),
        P("gx", "gy", None, None),
    )
    out_specs = P("gx", "gy", None, None, None, None)
    return jax.shard_map(
        per_device, mesh=mesh, in_specs=in_specs, out_specs=out_specs, check_vma=False
    )
```

profile of v0, /device:TPU:0, one launch (start us, length us, event | category | flops | bytes accessed | tf_op | source)
XLA Modules:
  0.0 316.9 jit_solution(7367842340995837070)
XLA Ops:
  0.0 0.7 fusion.30
  0.8 0.7 maximum_add_fusion
  1.6 0.8 fusion.33
  2.4 2.4 collective-permute-start
  4.8 1.3 collective-permute-start.1
  6.2 0.8 broadcast_select_fusion.2
  6.9 0.7 fusion.31
  7.7 0.8 select_reduce_fusion
  9.0 0.4 copy-done.4
  9.3 0.3 and_reduce_fusion
  10.0 4.1 %collective-permute-start.2 = (f32[4,4,1,128]{3,0,2,1:T(4,128)S(1)}, f32[4,4,1,128]{3,0,2,1:T(4,128)S(1)}, u32[]{:S(2)}, u32[]{:S(2)}) collective-permute-start(f32[4,4,1,128]{3,0,2,1:T(4,128)S(1)} %get-tuple-element.98), channel_id=1, source_target_pairs={{0,1},{1,2},{2,3},{4,5},{5,6},{6,7},{8,9},{9,10},{10,11},{12,13},{... | collective-permute-start | bytes 24584 | tf_op jit(solution)/shard_map/ppermute | solution.py:34
  14.1 1.3 collective-permute-start.3
  15.5 4.1 %collective-permute-done.3 = f32[4,4,1,128]{3,0,2,1:T(4,128)S(1)} collective-permute-done((f32[4,4,1,128]{3,0,2,1:T(4,128)S(1)}, f32[4,4,1,128]{3,0,2,1:T(4,128)S(1)}, u32[]{:S(2)}, u32[]{:S(2)}) %collective-permute-start.3) | collective-permute-done | bytes 8224 | tf_op jit(solution)/shard_map/ppermute | solution.py:35
  19.8 174.1 %gather_fusion = f32[16384]{0:T(1024)S(1)} fusion(f32[4,2,2,1152]{3,0,2,1:T(4,128)S(1)} %constant_dynamic-update-slice_fusion, s32[16384]{0:T(1024)S(1)} %bitcast.81), kind=kCustom, calls=%fused_computation | custom fusion | bytes 393216 | tf_op jit(solution)/shard_map/jvp(jit(take_along_axis))/gather | solution.py:80
  194.8 0.3 multiply_reduce_fusion.6
  195.5 96.6 %scatter_custom_fusion = f32[18432]{0:T(1024)S(1)} fusion(s32[16384]{0:T(1024)S(1)} %bitcast.104, f32[16384]{0:T(1024)S(1)} %bitcast.105, f32[]{:T(128)} %constant.181.clone.1), kind=kCustom, calls=%fused_computation.38 | custom fusion | flops 16384 | bytes 73732
  292.4 1.3 collective-permute-start.4
  293.7 4.5 %collective-permute-start.5 = (f32[3,4,128]{2,1,0:T(4,128)S(1)}, f32[3,4,128]{2,1,0:T(4,128)S(1)}, u32[]{:S(2)}, u32[]{:S(2)}) collective-permute-start(f32[3,4,128]{2,1,0:T(4,128)S(1)} %bitcast.107), channel_id=1, source_target_pairs={{0,1},{1,2},{2,3},{4,5},{5,6},{6,7},{8,9},{9,10},{10,11},{12,13},{... | collective-permute-start | bytes 18440 | tf_op jit(solution)/shard_map/ppermute | solution.py:24
  298.3 1.3 collective-permute-done.5
  299.6 1.3 collective-permute-start.6
  301.0 3.0 collective-permute-start.7
  304.1 0.7 collective-permute-done.7
  305.1 11.2 %all_to_all.5 = f32[4,2,7,128]{3,1,2,0:T(2,128)S(1)} all-to-all(f32[4,2,7,128]{3,1,2,0:T(2,128)S(1)} %fusion.20), channel_id=1, replica_groups=mesh['gx'=8,'gy'=4] {'gy'}, dimensions={0} | all-to-all | bytes 57344 | tf_op jit(solution)/shard_map/all_to_all | solution.py:151
  316.3 0.6 copy.187
  (98 shorter events, 2.8 us)
Async XLA Ops:
  0.0 6.1 %copy-start = (s32[8,2,2,128]{3,2,1,0:T(2,128)S(1)}, s32[8,2,2,128]{3,2,1,0:T(2,128)}, u32[]{:S(2)}) copy-start(s32[8,2,2,128]{3,2,1,0:T(2,128)} %param.20) | copy-start | bytes 49156
  1.6 7.1 %copy-start.5 = (s32[4]{0:T(128)S(1)}, s32[4]{0:T(128)}, u32[]{:S(2)}) copy-start(s32[4]{0:T(128)} %constant.255) | copy-start | bytes 52
  2.4 7.3 %collective-permute-start = (f32[4,1,2,128]{3,0,2,1:T(4,128)S(1)}, f32[4,1,2,128]{3,0,2,1:T(4,128)S(1)}, u32[]{:S(2)}, u32[]{:S(2)}) collective-permute-start(f32[4,1,2,128]{3,0,2,1:T(4,128)S(1)} %get-tuple-element.99), channel_id=1, source_target_pairs={{0,4},{4,8},{8,12},{12,16},{16,20},{20,24},{24,28},{1,5},{5,9},{9,... | collective-permute-start | bytes 12296 | tf_op jit(solution)/shard_map/ppermute | solution.py:34
  4.8 5.2 %collective-permute-start.1 = (f32[4,1,2,128]{3,0,2,1:T(4,128)S(1)}, f32[4,1,2,128]{3,0,2,1:T(4,128)S(1)}, u32[]{:S(2)}, u32[]{:S(2)}) collective-permute-start(f32[4,1,2,128]{3,0,2,1:T(4,128)S(1)} %get-tuple-element.100), channel_id=1, source_target_pairs={{4,0},{8,4},{12,8},{16,12},{20,16},{24,20},{28,24},{5,1},{9,5},{13... | collective-permute-start | bytes 12296 | tf_op jit(solution)/shard_map/ppermute | solution.py:35
  8.7 0.7 copy-start.4
  9.0 0.8 copy-start.3
  10.0 5.5 %collective-permute-start.2 = (f32[4,4,1,128]{3,0,2,1:T(4,128)S(1)}, f32[4,4,1,128]{3,0,2,1:T(4,128)S(1)}, u32[]{:S(2)}, u32[]{:S(2)}) collective-permute-start(f32[4,4,1,128]{3,0,2,1:T(4,128)S(1)} %get-tuple-element.98), channel_id=1, source_target_pairs={{0,1},{1,2},{2,3},{4,5},{5,6},{6,7},{8,9},{9,10},{10,11},{12,13},{... | collective-permute-start | bytes 24584 | tf_op jit(solution)/shard_map/ppermute | solution.py:34
  14.1 5.5 %collective-permute-start.3 = (f32[4,4,1,128]{3,0,2,1:T(4,128)S(1)}, f32[4,4,1,128]{3,0,2,1:T(4,128)S(1)}, u32[]{:S(2)}, u32[]{:S(2)}) collective-permute-start(f32[4,4,1,128]{3,0,2,1:T(4,128)S(1)} %get-tuple-element.97), channel_id=1, source_target_pairs={{1,0},{2,1},{3,2},{5,4},{6,5},{7,6},{9,8},{10,9},{11,10},{13,12},{... | collective-permute-start | bytes 24584 | tf_op jit(solution)/shard_map/ppermute | solution.py:35
  292.2 12.7 %copy-start.1 = (f32[3,2,2,128]{3,2,1,0:T(2,128)S(1)}, f32[3,2,2,128]{3,2,1,0:T(2,128)}, u32[]{:S(2)}) copy-start(f32[3,2,2,128]{3,2,1,0:T(2,128)} %param.17) | copy-start | bytes 18436
  292.2 12.7 %copy-start.2 = (f32[3,2,2,128]{3,2,1,0:T(2,128)S(1)}, f32[3,2,2,128]{3,2,1,0:T(2,128)}, u32[]{:S(2)}) copy-start(f32[3,2,2,128]{3,2,1,0:T(2,128)} %param.16) | copy-start | bytes 18436
  292.4 5.9 %collective-permute-start.4 = (f32[3,4,128]{2,1,0:T(4,128)S(1)}, f32[3,4,128]{2,1,0:T(4,128)S(1)}, u32[]{:S(2)}, u32[]{:S(2)}) collective-permute-start(f32[3,4,128]{2,1,0:T(4,128)S(1)} %bitcast.108), channel_id=1, source_target_pairs={{1,0},{2,1},{3,2},{5,4},{6,5},{7,6},{9,8},{10,9},{11,10},{13,12},{... | collective-permute-start | bytes 18440 | tf_op jit(solution)/shard_map/ppermute | solution.py:24
  293.7 5.9 %collective-permute-start.5 = (f32[3,4,128]{2,1,0:T(4,128)S(1)}, f32[3,4,128]{2,1,0:T(4,128)S(1)}, u32[]{:S(2)}, u32[]{:S(2)}) collective-permute-start(f32[3,4,128]{2,1,0:T(4,128)S(1)} %bitcast.107), channel_id=1, source_target_pairs={{0,1},{1,2},{2,3},{4,5},{5,6},{6,7},{8,9},{9,10},{10,11},{12,13},{... | collective-permute-start | bytes 18440 | tf_op jit(solution)/shard_map/ppermute | solution.py:24
  299.6 4.4 %collective-permute-start.6 = (f32[3,2,128]{2,1,0:T(2,128)S(1)}, f32[3,2,128]{2,1,0:T(2,128)S(1)}, u32[]{:S(2)}, u32[]{:S(2)}) collective-permute-start(f32[3,2,128]{2,1,0:T(2,128)S(1)} %bitcast.111), channel_id=1, source_target_pairs={{4,0},{8,4},{12,8},{16,12},{20,16},{24,20},{28,24},{5,1},{9,5},{13... | collective-permute-start | bytes 9224 | tf_op jit(solution)/shard_map/ppermute | solution.py:24
  301.0 3.8 %collective-permute-start.7 = (f32[3,2,128]{2,1,0:T(2,128)S(1)}, f32[3,2,128]{2,1,0:T(2,128)S(1)}, u32[]{:S(2)}, u32[]{:S(2)}) collective-permute-start(f32[3,2,128]{2,1,0:T(2,128)S(1)} %bitcast.112), channel_id=1, source_target_pairs={{0,4},{4,8},{8,12},{12,16},{16,20},{20,24},{24,28},{1,5},{5,9},{9,... | collective-permute-start | bytes 9224 | tf_op jit(solution)/shard_map/ppermute | solution.py:24
where the time goes:
time: 322 us; the launch traced here: 317 us
  local copies, waits for them, and re-layouts  176 us (55%)
  other arithmetic  103 us (32%)
  starting transfers between devices  19.2 us (6%)
  blocking collectives  11.2 us (3%)
  waiting for transfers between devices  6.4 us (2%)
    gather x2, local copies, waits for them, and re-layouts, gather_nearby(): picked = jnp.take_along_axis(joined, wide_index, axis=3)  174 us
    unnamed x7, other arithmetic  97.3 us
    all_to_all x1, blocking collectives, per_device(): lax.all_to_all(packed, 'gy', split_axis=0, concat_axis=0, tiled=True)  11.2 us
    ppermute x4, starting transfers between devices, shifted(): lax.ppermute(value, axis, [(source, source + steps) for source in range(f...  10.2 us
    ppermute x2, starting transfers between devices, extended(): before = lax.ppermute(last, axis, up)  6.5 us
  transfers between devices with their start and end apart: 8, of which 4 were waited for; matrix products, arithmetic and copies ran while one was open for 1% of the time, Pallas kernels for 0%

commit v1 on v0

v1 whole, which is shorter than its diff:
```python
import functools

import jax
import jax.numpy as jnp
from jax import lax
from jax.experimental import pallas as pl
from jax.experimental.pallas import tpu as pltpu
from jax.sharding import PartitionSpec as P

repulse_a = 1830.8
attract_b = 471.18
decay_one = 2.4799
decay_two = 1.7322
beta_t = 1.1e-06
expo_n = 0.78734
coeff_c2 = 100390.0**2
coeff_d2 = 16.217**2
coeff_h = -0.59825
spacing = 2.4
time_step = 0.001
half_step = 0.0005
force_scale = 9648.53 / 28.0855
far_away = 1.0e6
half_pi = 1.5707963267948966
ROWS = 8

VMEM = pltpu.MemorySpace.VMEM
SMEM = pltpu.MemorySpace.SMEM


def line_partner(place, count, odd):
    other = ((place - 1) ^ 1) + 1 if odd else place ^ 1
    return other if 0 <= other < count else None


def exchange_pairs(counts, axis, odd):
    pairs = []
    for a in range(counts[0]):
        for b in range(counts[1]):
            here = [a, b]
            other = line_partner(here[axis], counts[axis], odd)
            if other is not None:
                here[axis] = other
            else:
                spare = line_partner(here[1 - axis], counts[1 - axis], False)
                if spare is None:
                    continue
                here[1 - axis] = spare
            pairs.append((a * counts[1] + b, here[0] * counts[1] + here[1]))
    return pairs


def round_partner(place, turn, count):
    ring = count - 1
    other = lax.rem(turn - place + 2 * ring, ring)
    alone = turn * ((ring + 1) // 2) % ring
    return jnp.where(place == ring, alone, jnp.where(place == alone, ring, other))


def round_pairs(counts, turn):
    ring = counts[1] - 1
    alone = turn * ((ring + 1) // 2) % ring
    pairs = []
    for a in range(counts[0]):
        for b in range(counts[1]):
            other = alone if b == ring else ring if b == alone else (turn - b) % ring
            pairs.append((a * counts[1] + b, a * counts[1] + other))
    return pairs


def prepare_kernel(disp, vel, force, heights, counts, lists, plan, rows, send_a, send_b, *, capacity):
    _, cells_x, cells_y, slots = disp.shape
    entries = lists.shape[0]
    at_x, at_y = lax.axis_index("gx"), lax.axis_index("gy")
    even_x = lax.rem(at_x, 2) == 0
    for x in range(cells_x):
        base_x = ((at_x * cells_x + x).astype(jnp.float32) + 0.5) * spacing
        for y in range(cells_y):
            base_y = ((at_y * cells_y + y).astype(jnp.float32) + 0.5) * spacing
            layer = heights[x, pl.ds(y, 1), :]
            occupied = (layer < counts[x, y]).astype(jnp.float32)
            lattice = (base_x, base_y, (layer.astype(jnp.float32) + 0.5) * spacing)
            column = (x * cells_y + y) * ROWS
            for q in range(3):
                pick = (q, x, pl.ds(y, 1), slice(None))
                speed = vel[pick] + half_step * (force[pick] * force_scale)
                offset = disp[pick] + time_step * speed
                rows[pl.ds(column + q, 1), :] = offset
                rows[pl.ds(column + 3 + q, 1), :] = speed
                point = lattice[q] + offset
                place = (q * cells_y + y) * cells_x + x
                send_a[pl.ds(place, 1), :] = point
                send_b[pl.ds(place, 1), :] = point
            rows[pl.ds(column + 6, 1), :] = occupied
            owner = plan[x * cells_y + y]
            earlier = 0
            for c in range(x * cells_y + y):
                earlier = earlier + (plan[c] == owner).astype(jnp.int32)
            rows[pl.ds(column + 7, 1), :] = jnp.full(
                (1, slots), (owner * capacity + earlier).astype(jnp.float32)
            )
            place = (3 * cells_y + y) * cells_x + x
            send_a[pl.ds(place, 1), :] = occupied
            send_b[pl.ds(place, 1), :] = occupied
    base = 4 * cells_y * cells_x
    for m in range(entries):
        low = lists[m, 0].astype(jnp.float32)
        high = lists[m, cells_x - 1].astype(jnp.float32)
        send_a[pl.ds(base + m * cells_y, cells_y), :] = jnp.where(even_x, high, low)
        send_b[pl.ds(base + m * cells_y, cells_y), :] = jnp.where(even_x, low, high)


def strip_kernel(rows, own, got_a, got_b, middle, send_c, send_d, *, count_x, cells_x, cells_y):
    at_x, at_y = lax.axis_index("gx"), lax.axis_index("gy")
    even_x, even_y = lax.rem(at_x, 2) == 0, lax.rem(at_y, 2) == 0
    has_left = (at_x > 0).astype(jnp.float32)
    has_right = (at_x < count_x - 1).astype(jnp.float32)
    wide = cells_x + 4
    for q in range(4):
        for y in range(cells_y):
            place = (q * cells_y + y) * cells_x
            take = lambda ref: ref[pl.ds(place, cells_x), :]
            left = jnp.where(even_x, take(got_b), take(got_a))[cells_x - 2 :]
            right = jnp.where(even_x, take(got_a), take(got_b))[:2]
            if q == 3:
                left, right = left * has_left, right * has_right
            strip = jnp.concatenate([left, take(own), right], axis=0)
            middle[q, y] = strip
        low, high = middle[q, 0], middle[q, cells_y - 1]
        send_c[pl.ds(q * wide, wide), :] = jnp.where(even_y, high, low)
        send_d[pl.ds(q * wide, wide), :] = jnp.where(even_y, low, high)
    for x in range(cells_x):
        low = rows[pl.ds(x * cells_y * ROWS + 7, 1), :]
        high = rows[pl.ds((x * cells_y + cells_y - 1) * ROWS + 7, 1), :]
        send_c[pl.ds(4 * wide + x, 1), :] = jnp.where(even_y, high, low)
        send_d[pl.ds(4 * wide + x, 1), :] = jnp.where(even_y, low, high)


def half_wave(radius):
    angle = half_pi * (jnp.clip(radius, 2.7, 3.0) - 2.85) / 0.15
    square = angle * angle
    sine, cosine = 0.0, 0.0
    for odd in (15, 13, 11, 9, 7, 5, 3, 1):
        factor_s = 1.0
        for n in range(2, odd + 1):
            factor_s /= n
        factor_c = factor_s * odd
        sign = -1.0 if odd % 4 == 3 else 1.0
        sine = sine * square + sign * factor_s
        cosine = cosine * square + sign * factor_c
    return sine * angle, cosine


def step_gate(value):
    return jnp.where(value > 1.0, 1.0, jnp.where(value == 1.0, 0.5, 0.0))


def column_gradients(center, occupied, nearby):
    entries = len(nearby)
    each = range(entries)
    inverse, gate_r, weight, slope, unit, repulse, attract = [], [], [], [], [], [], []
    for m in each:
        offset = [nearby[m][q] - center[q] for q in range(3)]
        square = offset[0] * offset[0] + offset[1] * offset[1] + offset[2] * offset[2]
        bounded = jnp.maximum(square, 1.0)
        radius = jnp.sqrt(bounded)
        inverse.append(1.0 / radius)
        gate_r.append(step_gate(square))
        sine, cosine = half_wave(radius)
        inside, outside = radius < 2.7, radius > 3.0
        weight.append(jnp.where(inside, 1.0, jnp.where(outside, 0.0, 0.5 - 0.5 * sine)))
        slope.append(jnp.where(inside | outside, 0.0, (-0.5 * half_pi / 0.15) * cosine))
        unit.append([offset[q] * inverse[m] for q in range(3)])
        repulse.append(repulse_a * jnp.exp(-decay_one * radius))
        attract.append(attract_b * jnp.exp(-decay_two * radius))
    zero = jnp.zeros_like(occupied)
    total = [zero for _ in each]
    angular, tilt = {}, {}
    for m in each:
        for k in range(m + 1, entries):
            cosine = sum(unit[m][q] * unit[k][q] for q in range(3))
            lean = coeff_h - cosine
            spread = lean * lean
            part = 1.0 / (coeff_d2 + spread)
            value = 1.0 + (coeff_c2 / coeff_d2) * (spread * part)
            angular[m, k] = value
            tilt[m, k] = (-2.0 * coeff_c2) * lean * (part * part)
            total[m] = total[m] + weight[k] * value
            total[k] = total[k] + weight[m] * value
    half = 0.5 * occupied
    pull, by_weight, by_radius = [], [], []
    for m in each:
        bond_sum = jnp.maximum(total[m], 1.0)
        power = jnp.exp(expo_n * jnp.log(beta_t * bond_sum))
        bond = jnp.exp((-0.5 / expo_n) * jnp.log(1.0 + power))
        loss = 0.5 * bond * power / ((1.0 + power) * bond_sum)
        pull.append(half * weight[m] * attract[m] * loss * step_gate(total[m]))
        by_weight.append(half * (repulse[m] - attract[m] * bond))
        by_radius.append(
            half * weight[m] * (decay_two * attract[m] * bond - decay_one * repulse[m])
        )
    by_unit = [[zero] * 3 for _ in each]
    for m in each:
        for k in range(m + 1, entries):
            by_weight[m] = by_weight[m] + pull[k] * angular[m, k]
            by_weight[k] = by_weight[k] + pull[m] * angular[m, k]
            turn = (pull[m] * weight[k] + pull[k] * weight[m]) * tilt[m, k]
            for q in range(3):
                by_unit[m][q] = by_unit[m][q] + turn * unit[k][q]
                by_unit[k][q] = by_unit[k][q] + turn * unit[m][q]
    grads = []
    for m in each:
        across = [by_unit[m][q] * inverse[m] for q in range(3)]
        along = sum(across[q] * unit[m][q] for q in range(3))
        reach = gate_r[m] * (by_radius[m] + by_weight[m] * slope[m] - along)
        grads.append([across[q] + unit[m][q] * reach for q in range(3)])
    return grads


def force_kernel(
    rows, middle, got_a, got_b, got_c, got_d, lists, plan, *refs, counts, cells_x, cells_y, capacity, turns
):
    outs = refs[: len(turns) + 1] if turns else refs[:1]
    table, index, parts, hot, left_side, main, ghost = refs[len(outs) :]
    entries, slots = lists.shape[0], lists.shape[3]
    shift = slots.bit_length() - 1
    at_x, at_y = lax.axis_index("gx"), lax.axis_index("gy")
    even_x, even_y = lax.rem(at_x, 2) == 0, lax.rem(at_y, 2) == 0
    wide, near = cells_x + 4, cells_x + 2
    centers = near * cells_y
    base = 4 * cells_x * cells_y
    for m in range(entries):
        here = pl.ds(base + m * cells_y, cells_y)
        left = jnp.where(even_x, got_b[here, :], got_a[here, :]).astype(jnp.int32)
        right = jnp.where(even_x, got_a[here, :], got_b[here, :]).astype(jnp.int32)
        for y in range(cells_y):
            index[m, pl.ds(y * near, 1), :] = left[y : y + 1]
            for x in range(cells_x):
                index[m, pl.ds(y * near + 1 + x, 1), :] = lists[m, x, pl.ds(y, 1), :]
            index[m, pl.ds(y * near + near - 1, 1), :] = right[y : y + 1]
    has_below, has_above = at_y > 0, at_y < counts[1] - 1
    strips = []
    for y in range(-1, cells_y + 1):
        if 0 <= y < cells_y:
            strip = [middle[q, y] for q in range(4)]
        else:
            swap, there = (even_y, has_below) if y < 0 else (jnp.logical_not(even_y), has_above)
            strip = [
                jnp.where(swap, got_d[pl.ds(q * wide, wide), :], got_c[pl.ds(q * wide, wide), :])
                for q in range(4)
            ]
            strip[3] = strip[3] * there.astype(jnp.float32)
        strip[2] = jnp.where(strip[3] > 0.0, strip[2], far_away)
        for move in range(3):
            for q in range(4):
                table[q, move, pl.ds((y + 1) * near, near), :] = strip[q][move : move + near]
    center = [table[q, 1, pl.ds(near, centers), :] for q in range(4)]
    occupied = center[3]
    entry_slot, entry_cell = [], []
    for m in range(entries):
        value = index[m]
        entry_slot.append(value & (slots - 1))
        entry_cell.append(value >> shift)
    nearby = [[None] * 3 for _ in range(entries)]
    for q in range(3):
        for c in range(9):
            source = table[q, c // 3, pl.ds((c % 3) * near, centers), :]
            for m in range(entries):
                picked = jnp.take_along_axis(
                    source, entry_slot[m], axis=1, mode="promise_in_bounds"
                )
                nearby[m][q] = (
                    picked if c == 0 else jnp.where(entry_cell[m] == c, picked, nearby[m][q])
                )
    grads = column_gradients(center[:3], occupied, nearby)
    own = [sum(grads[m][q] for m in range(entries)) for q in range(3)]
    for m in range(entries):
        index[m] = entry_slot[m]
        for q in range(3):
            high = grads[m][q].astype(jnp.bfloat16).astype(jnp.float32)
            parts[m, 3 + q] = high
            parts[m, q] = grads[m][q] - high
        parts[m, 6] = entry_cell[m].astype(jnp.float32)
        parts[m, 7] = jnp.zeros_like(occupied)
    for q in range(3):
        parts[entries, q] = jnp.zeros_like(occupied)
        parts[entries, 3 + q] = own[q]
    for q in (6, 7):
        parts[entries, q] = jnp.zeros_like(occupied)
    reached = {}
    ramp = lax.broadcasted_iota(jnp.int32, (slots, slots), 0)
    for y in range(cells_y):
        for x in range(-1, cells_x + 1):
            i = y * near + x + 1
            targets = [
                (dx, dy) for dx in (-1, 0, 1) if 0 <= x + dx < cells_x for dy in (-1, 0, 1)
            ]
            for m in range(entries):
                lanes = pl.ds(m * slots, slots)
                row = jnp.broadcast_to(index[m, pl.ds(i, 1), :], (slots, slots))
                hot[:, lanes] = jnp.where(ramp == row, 1.0, 0.0).astype(jnp.bfloat16)
                values = parts[m, :, i, :]
                cell = jnp.broadcast_to(parts[m, 6, pl.ds(i, 1), :], (ROWS, slots))
                masked = []
                for dx, dy in targets:
                    c = (dx + 1) * 3 + dy + 1
                    masked.append(jnp.where(cell == float(c), values, 0.0))
                left_side[pl.ds(0, ROWS * len(targets)), lanes] = jnp.concatenate(
                    masked, axis=0
                ).astype(jnp.bfloat16)
            sums = lax.dot_general(
                left_side[pl.ds(0, ROWS * len(targets)), :],
                hot[...],
                (((1,), (1,)), ((), ())),
                preferred_element_type=jnp.float32,
            )
            for n, (dx, dy) in enumerate(targets):
                key = (x + dx, y + dy)
                block = sums[n * ROWS : (n + 1) * ROWS]
                reached[key] = block if key not in reached else reached[key] + block
    line = lax.broadcasted_iota(jnp.int32, (ROWS, slots), 0)
    kick = half_step * force_scale
    chosen = (line >= 3) & (line < 6)
    main[...] = jnp.zeros_like(main)
    for x in range(cells_x):
        for y in range(-1, cells_y + 1):
            block = reached[x, y]
            block = block + pltpu.roll(block, 3, 0)
            if 0 <= y < cells_y:
                block = parts[entries, :, y * near + x + 1, :] - block
                column = rows[pl.ds((x * cells_y + y) * ROWS, ROWS), :]
                column = column + jnp.where(chosen, kick * block, 0.0)
                owner = plan[x * cells_y + y]
                earlier = 0
                for c in range(x * cells_y + y):
                    earlier = earlier + (plan[c] == owner).astype(jnp.int32)
                main[owner, pl.ds(earlier * 7, 7), :] = column[:7]
            else:
                ghost[0 if y < 0 else 1, x] = -kick * block
    places = [4 * wide + x for x in range(cells_x)]
    below = [jnp.where(even_y, got_d[pl.ds(p, 1), :], got_c[pl.ds(p, 1), :]) for p in places]
    above = [jnp.where(even_y, got_c[pl.ds(p, 1), :], got_d[pl.ds(p, 1), :]) for p in places]
    size = main.shape[1]

    def message(owner):
        pieces = [main[owner]]
        for side, named in enumerate((below, above)):
            for slot in range(capacity):
                wanted = (owner * capacity + slot).astype(jnp.float32)
                piece = 0.0
                for x in range(cells_x):
                    piece = piece + jnp.where(named[x] == wanted, ghost[side, x, pl.ds(3, 3), :], 0.0)
                pieces.append(piece)
        return pieces

    def write(ref, pieces):
        first = 0
        for piece in pieces:
            ref[pl.ds(first, piece.shape[0]), :] = piece
            first += piece.shape[0]

    if turns:
        for ref, turn in zip(outs[:-1], turns):
            write(ref, message(round_partner(at_y, turn, counts[1])))
        write(outs[-1], message(at_y))
    else:
        for owner in range(counts[1]):
            write(outs[0].at[owner], message(jnp.int32(owner)))


def gather_kernel(*refs, count, capacity, turns):
    at_y = lax.axis_index("gy")
    if turns:
        ins, out, held = refs[:-2], refs[-2], refs[-1]
        for ref, turn in zip(ins[:-1], turns):
            held[round_partner(at_y, turn, count)] = ref[...]
        held[at_y] = ins[-1][...]
    else:
        held, out = refs
    first = capacity * 7
    for source in range(count):
        for slot in range(capacity):
            block = held[source, pl.ds(slot * 7, 7), :]
            speed = block[3:6]
            if source + 1 < count:
                speed = speed + held[source + 1, pl.ds(first + slot * 3, 3), :]
            if source > 0:
                speed = speed + held[source - 1, pl.ds(first + (capacity + slot) * 3, 3), :]
            out[source, slot, pl.ds(0, 3), :] = block[:3]
            out[source, slot, pl.ds(3, 3), :] = speed
            out[source, slot, pl.ds(6, 1), :] = block[6:7]


def per_device(displacement, velocity, forces, heights, counts, neighbours, plan):
    cells_x, cells_y, slots = heights.shape
    entries = neighbours.shape[0]
    sizes = (lax.axis_size("gx"), lax.axis_size("gy"))
    columns = cells_x * cells_y
    capacity = max(2, (2 * columns + sizes[1] - 1) // sizes[1])
    owners = plan.reshape(columns)
    whole, scalar = pl.BlockSpec(memory_space=VMEM), pl.BlockSpec(memory_space=SMEM)
    shape = lambda *dims: jax.ShapeDtypeStruct(dims, jnp.float32)
    wide, near = cells_x + 4, cells_x + 2
    centers = near * cells_y

    def swap(value, pairs):
        return lax.ppermute(value, ("gx", "gy"), pairs)

    first_size = 4 * columns + entries * cells_y
    rows, send_a, send_b = pl.pallas_call(
        functools.partial(prepare_kernel, capacity=capacity),
        out_shape=(shape(columns * ROWS, slots), shape(first_size, slots), shape(first_size, slots)),
        in_specs=[whole, whole, whole, whole, scalar, whole, scalar],
        out_specs=(whole, whole, whole),
        name="prepare",
    )(displacement, velocity, forces, heights, counts, neighbours, owners)
    got_a = swap(send_a, exchange_pairs(sizes, 0, False))
    got_b = swap(send_b, exchange_pairs(sizes, 0, True))
    second_size = 4 * wide + cells_x
    middle, send_c, send_d = pl.pallas_call(
        functools.partial(strip_kernel, count_x=sizes[0], cells_x=cells_x, cells_y=cells_y),
        out_shape=(shape(4, cells_y, wide, slots), shape(second_size, slots), shape(second_size, slots)),
        in_specs=[whole] * 4,
        out_specs=(whole, whole, whole),
        name="strips",
    )(rows, send_a, got_a, got_b)
    got_c = swap(send_c, exchange_pairs(sizes, 1, False))
    got_d = swap(send_d, exchange_pairs(sizes, 1, True))
    turns = tuple(range(sizes[1] - 1)) if sizes[1] in (2, 4) else ()
    size = capacity * 13
    out_shape = (shape(size, slots),) * (len(turns) + 1) if turns else (shape(sizes[1], size, slots),)
    sent = pl.pallas_call(
        functools.partial(
            force_kernel, counts=sizes, cells_x=cells_x, cells_y=cells_y, capacity=capacity, turns=turns
        ),
        out_shape=out_shape,
        in_specs=[whole] * 7 + [scalar],
        out_specs=tuple(whole for _ in out_shape),
        scratch_shapes=[
            pltpu.VMEM((4, 3, near * (cells_y + 2), slots), jnp.float32),
            pltpu.VMEM((entries, centers, slots), jnp.int32),
            pltpu.VMEM((entries + 1, ROWS, centers, slots), jnp.float32),
            pltpu.VMEM((slots, entries * slots), jnp.bfloat16),
            pltpu.VMEM((9 * ROWS, entries * slots), jnp.bfloat16),
            pltpu.VMEM((sizes[1], capacity * 7, slots), jnp.float32),
            pltpu.VMEM((2, cells_x, ROWS, slots), jnp.float32),
        ],
        name="forces",
    )(rows, middle, got_a, got_b, got_c, got_d, neighbours, owners)
    if turns:
        arrived = [swap(value, round_pairs(sizes, turn)) for value, turn in zip(sent, turns)]
        arrived.append(sent[-1])
        scratch = [pltpu.VMEM((sizes[1], size, slots), jnp.float32)]
    else:
        arrived = [lax.all_to_all(sent[0], "gy", split_axis=0, concat_axis=0, tiled=True)]
        scratch = []
    result = pl.pallas_call(
        functools.partial(gather_kernel, count=sizes[1], capacity=capacity, turns=turns),
        out_shape=shape(sizes[1], capacity, 7, slots),
        in_specs=[whole] * len(arrived),
        out_specs=whole,
        scratch_shapes=scratch,
        name="collect",
    )(*arrived)
    return result[None, None]


def solution(mesh):
    in_specs = (
        P(None, "gx", "gy", None),
        P(None, "gx", "gy", None),
        P(None, "gx", "gy", None),
        P("gx", "gy", None),
        P("gx", "gy"),
        P(None, "gx", "gy", None),
        P("gx", "gy", None, None),
    )
    out_specs = P("gx", "gy", None, None, None, None)
    return jax.shard_map(
        per_device, mesh=mesh, in_specs=in_specs, out_specs=out_specs, check_vma=False
    )
```

time: 322 us -> 30.8 us (0.10); the launches traced: 317 us -> 30.3 us
  local copies, waits for them, and re-layouts: 176 us -> 3.2 us
  other arithmetic: 103 us -> 0 us
  blocking collectives: 11.2 us -> 0 us
  starting transfers between devices: 19.2 us -> 10.3 us
  Pallas kernels: 0 us -> 8.18 us
    gather x2 -> x0, local copies, waits for them, and re-layouts: 174 us -> none  [gather_nearby(): picked = jnp.take_along_axis(joined, wide_index, axis=3)]
    unnamed x7 -> x0, other arithmetic: 97.3 us -> none
    all_to_all x1 -> x0, blocking collectives: 11.2 us -> none  [per_device(): lax.all_to_all(packed, 'gy', split_axis=0, concat_axis=0, tiled=True)]
    ppermute x8 -> x7, starting transfers between devices: 19.2 us -> 10.3 us  [swap(): return lax.ppermute(value, ('gx', 'gy'), pairs)]
    pallas_call x0 -> x4, Pallas kernels: none -> 8.18 us  [the longest x1 3.89 us: per_device(): pl.pallas_call(functools.partial(force_kernel, counts=sizes, cells_x=cell...]
    ppermute x8 -> x7, waiting for transfers between devices: 6.4 us -> 8.66 us  [swap(): return lax.ppermute(value, ('gx', 'gy'), pairs)]
  transfers between devices with their start and end apart: 8 -> 7, of which waited for: 4 -> 5; matrix products, arithmetic and copies ran while one was open for 1% -> 0% of each run, Pallas kernels for 0% -> 0%
where the time goes in v1:
time: 30.8 us; the launch traced here: 30.3 us
  starting transfers between devices  10.3 us (33%)
  waiting for transfers between devices  8.66 us (28%)
  Pallas kernels  8.18 us (27%)
  local copies, waits for them, and re-layouts  3.2 us (10%)
    ppermute x7, starting transfers between devices, swap(): return lax.ppermute(value, ('gx', 'gy'), pairs)  10.3 us
    ppermute x7, waiting for transfers between devices, swap(): return lax.ppermute(value, ('gx', 'gy'), pairs)  8.66 us
    pallas_call x1, Pallas kernels, per_device(): pl.pallas_call(functools.partial(force_kernel, counts=sizes, cells_x=cell...  3.89 us
    unnamed x14, local copies, waits for them, and re-layouts  1.82 us
    pallas_call x1, Pallas kernels, per_device(): pl.pallas_call(functools.partial(prepare_kernel, capacity=capacity), out_...  1.49 us
    pallas_call x1, Pallas kernels, per_device(): pl.pallas_call(functools.partial(strip_kernel, count_x=sizes[0], cells_x=...  1.4 us
    pallas_call x1, Pallas kernels, per_device(): pl.pallas_call(functools.partial(gather_kernel, count=sizes[1], capacity=...  1.4 us
    broadcast_in_dim x1, local copies, waits for them, and re-layouts, per_device(): return result[None, None]  1.38 us
  transfers between devices with their start and end apart: 7, of which 5 were waited for; matrix products, arithmetic and copies ran while one was open for 0% of the time, Pallas kernels for 0%

profile of v1, /device:TPU:0, one launch (start us, length us, event | category | flops | bytes accessed | tf_op | source)
XLA Modules:
  0.0 30.3 jit_solution(92231171288490577)
XLA Ops:
  0.0 1.5 %prepare.1 = (f32[32,128]{1,0:T(8,128)}, f32[32,128]{1,0:T(8,128)}, f32[32,128]{1,0:T(8,128)}) custom-call(f32[3,2,2,128]{3,2,1,0:T(2,128)} %disp.1, f32[3,2,2,128]{3,2,1,0:T(2,128)} %vel.1, f32[3,2,2,128]{3,2,1,0:T(2,128)} %force.1, s32[2,2,128]{2,1,0:T(2,128)} %heights.1, s32[2,2]{1,0:T(2,128)} %counts.1, s32[8,2,2,128]{3,2,1,0:T(2,128)} %lists.3, s32[4]{0:T(128)} %bitcast.3), custom_call_target="tpu_custom_call" | custom-call | tf_op jit(solution)/shard_map/prepare/pallas_call | solution.py:410
  1.5 3.1 %collective-permute-start.1 = (f32[32,128]{1,0:T(8,128)}, f32[32,128]{1,0:T(8,128)S(1)}, u32[]{:S(2)}, u32[]{:S(2)}) collective-permute-start(f32[32,128]{1,0:T(8,128)} %get-tuple-element.17), channel_id=1, source_target_pairs={{0,1},{1,0},{2,3},{3,2},{4,8},{5,9},{6,10},{7,11},{8,4},{9,5},{10,... | collective-permute-start | bytes 49160 | tf_op jit(solution)/shard_map/ppermute | solution.py:407
  4.5 0.0 collective-permute-start
  4.6 1.9 %collective-permute-done.1.got_b = f32[32,128]{1,0:T(8,128)S(1)} collective-permute-done((f32[32,128]{1,0:T(8,128)}, f32[32,128]{1,0:T(8,128)S(1)}, u32[]{:S(2)}, u32[]{:S(2)}) %collective-permute-start.1) | collective-permute-done | bytes 16416 | tf_op jit(solution)/shard_map/ppermute | solution.py:407
  6.5 0.0 collective-permute-done.got_a
  6.5 0.6 %copy-done = f32[32,128]{1,0:T(8,128)} copy-done((f32[32,128]{1,0:T(8,128)}, f32[32,128]{1,0:T(8,128)S(1)}, u32[]{:S(2)}) %copy-start) | copy-done | bytes 16408
  7.1 0.0 copy-done.1
  7.1 1.4 %strips.1 = (f32[4,2,6,128]{3,2,1,0:T(8,128)}, f32[26,128]{1,0:T(8,128)}, f32[26,128]{1,0:T(8,128)}) custom-call(f32[32,128]{1,0:T(8,128)} %get-tuple-element.15.rows, f32[32,128]{1,0:T(8,128)} %get-tuple-element.16.own, f32[32,128]{1,0:T(8,128)} %copy-done.1, f32[32,128]{1,0:T(8,128)} %copy-done), custom_call_target="tpu_custom_call" | custom-call | tf_op jit(solution)/shard_map/strips/pallas_call | solution.py:420
  8.5 2.0 %collective-permute-start.2 = (f32[26,128]{1,0:T(8,128)}, f32[26,128]{1,0:T(8,128)S(1)}, u32[]{:S(2)}, u32[]{:S(2)}) collective-permute-start(f32[26,128]{1,0:T(8,128)} %get-tuple-element.19), channel_id=1, source_target_pairs={{0,1},{1,0},{2,3},{3,2},{4,5},{5,4},{6,7},{7,6},{8,9},{9,8},{10,11... | collective-permute-start | bytes 39944 | tf_op jit(solution)/shard_map/ppermute | solution.py:407
  10.5 0.0 collective-permute-start.3
  10.5 1.9 %collective-permute-done.2.got_c = f32[26,128]{1,0:T(8,128)S(1)} collective-permute-done((f32[26,128]{1,0:T(8,128)}, f32[26,128]{1,0:T(8,128)S(1)}, u32[]{:S(2)}, u32[]{:S(2)}) %collective-permute-start.2) | collective-permute-done | bytes 13344 | tf_op jit(solution)/shard_map/ppermute | solution.py:407
  12.4 0.0 collective-permute-done.3.got_d
  12.4 0.6 %copy-done.5 = f32[26,128]{1,0:T(8,128)} copy-done((f32[26,128]{1,0:T(8,128)}, f32[26,128]{1,0:T(8,128)S(1)}, u32[]{:S(2)}) %copy-start.5) | copy-done | bytes 13336
  13.0 0.0 copy-done.6
  13.0 3.9 %forces.1 = (f32[26,128]{1,0:T(8,128)}, f32[26,128]{1,0:T(8,128)}, f32[26,128]{1,0:T(8,128)}, f32[26,128]{1,0:T(8,128)}) custom-call(f32[32,128]{1,0:T(8,128)} %get-tuple-element.15.rows, f32[4,2,6,128]{3,2,1,0:T(8,128)} %get-tuple-element.18.middle, f32[32,128]{1,0:T(8,128)} %copy-done.1, f32[32,128]{1,0:T(8,128)} %copy-done, f32[26,128]{1,0:T(8,128)} %copy-done.5, ...), custom_call_target="tpu_custom_call" | custom-call | tf_op jit(solution)/shard_map/forces/pallas_call | solution.py:432
  16.9 4.0 %collective-permute-start.4 = (f32[26,128]{1,0:T(8,128)}, f32[26,128]{1,0:T(8,128)S(1)}, u32[]{:S(2)}, u32[]{:S(2)}) collective-permute-start(f32[26,128]{1,0:T(8,128)} %get-tuple-element.21), channel_id=1, source_target_pairs={{0,3},{1,2},{2,1},{3,0},{4,7},{5,6},{6,5},{7,4},{8,11},{9,10},{10,... | collective-permute-start | bytes 39944 | tf_op jit(solution)/shard_map/ppermute | solution.py:407
  21.0 1.1 %collective-permute-start.5 = (f32[26,128]{1,0:T(8,128)}, f32[26,128]{1,0:T(8,128)S(1)}, u32[]{:S(2)}, u32[]{:S(2)}) collective-permute-start(f32[26,128]{1,0:T(8,128)} %get-tuple-element.22), channel_id=1, source_target_pairs={{0,1},{1,0},{2,3},{3,2},{4,5},{5,4},{6,7},{7,6},{8,9},{9,8},{10,11... | collective-permute-start | bytes 39944 | tf_op jit(solution)/shard_map/ppermute | solution.py:407
  22.1 0.0 collective-permute-start.6
  22.1 0.8 %collective-permute-done.4.refs_0_ = f32[26,128]{1,0:T(8,128)S(1)} collective-permute-done((f32[26,128]{1,0:T(8,128)}, f32[26,128]{1,0:T(8,128)S(1)}, u32[]{:S(2)}, u32[]{:S(2)}) %collective-permute-start.4) | collective-permute-done | bytes 13344 | tf_op jit(solution)/shard_map/ppermute | solution.py:407
  22.9 2.0 %collective-permute-done.5.refs_1_ = f32[26,128]{1,0:T(8,128)S(1)} collective-permute-done((f32[26,128]{1,0:T(8,128)}, f32[26,128]{1,0:T(8,128)S(1)}, u32[]{:S(2)}, u32[]{:S(2)}) %collective-permute-start.5) | collective-permute-done | bytes 13344 | tf_op jit(solution)/shard_map/ppermute | solution.py:407
  24.9 2.0 %collective-permute-done.6.refs_2_ = f32[26,128]{1,0:T(8,128)S(1)} collective-permute-done((f32[26,128]{1,0:T(8,128)}, f32[26,128]{1,0:T(8,128)S(1)}, u32[]{:S(2)}, u32[]{:S(2)}) %collective-permute-start.6) | collective-permute-done | bytes 13344 | tf_op jit(solution)/shard_map/ppermute | solution.py:407
  27.0 0.6 %copy-done.4 = f32[26,128]{1,0:T(8,128)} copy-done((f32[26,128]{1,0:T(8,128)}, f32[26,128]{1,0:T(8,128)S(1)}, u32[]{:S(2)}) %copy-start.4) | copy-done | bytes 13336
  27.6 1.4 %collect.1 = f32[4,2,7,128]{3,2,1,0:T(8,128)} custom-call(f32[26,128]{1,0:T(8,128)} %copy-done.2, f32[26,128]{1,0:T(8,128)} %copy-done.3, f32[26,128]{1,0:T(8,128)} %copy-done.4, f32[26,128]{1,0:T(8,128)} %get-tuple-element.24.refs_3_), custom_call_target="tpu_custom_call" | custom-call | tf_op jit(solution)/shard_map/collect/pallas_call | solution.py:457
  29.0 1.4 %copy.8 = f32[1,1,4,2,7,128]{5,3,4,2,1,0:T(2,128)} copy(f32[1,1,4,2,7,128]{5,4,3,2,1,0:T(8,128)} %bitcast.2) | data formatting | bytes 57344 | tf_op jit(solution)/shard_map/broadcast_in_dim | solution.py:465
  (9 shorter events, 0.0 us)
Async XLA Ops:
  1.5 5.0 %collective-permute-start.1 = (f32[32,128]{1,0:T(8,128)}, f32[32,128]{1,0:T(8,128)S(1)}, u32[]{:S(2)}, u32[]{:S(2)}) collective-permute-start(f32[32,128]{1,0:T(8,128)} %get-tuple-element.17), channel_id=1, source_target_pairs={{0,1},{1,0},{2,3},{3,2},{4,8},{5,9},{6,10},{7,11},{8,4},{9,5},{10,... | collective-permute-start | bytes 49160 | tf_op jit(solution)/shard_map/ppermute | solution.py:407
  4.5 1.9 %collective-permute-start = (f32[32,128]{1,0:T(8,128)}, f32[32,128]{1,0:T(8,128)S(1)}, u32[]{:S(2)}, u32[]{:S(2)}) collective-permute-start(f32[32,128]{1,0:T(8,128)} %get-tuple-element.16.own), channel_id=1, source_target_pairs={{0,4},{1,5},{2,6},{3,7},{4,0},{5,1},{6,2},{7,3},{8,12},{9,13},{10,... | collective-permute-start | bytes 49160 | tf_op jit(solution)/shard_map/ppermute | solution.py:407
  6.5 0.6 %copy-start = (f32[32,128]{1,0:T(8,128)}, f32[32,128]{1,0:T(8,128)S(1)}, u32[]{:S(2)}) copy-start(f32[32,128]{1,0:T(8,128)S(1)} %collective-permute-done.1.got_b) | copy-start | bytes 49156
  6.5 0.6 %copy-start.1 = (f32[32,128]{1,0:T(8,128)}, f32[32,128]{1,0:T(8,128)S(1)}, u32[]{:S(2)}) copy-start(f32[32,128]{1,0:T(8,128)S(1)} %collective-permute-done.got_a) | copy-start | bytes 49156
  8.5 3.9 %collective-permute-start.2 = (f32[26,128]{1,0:T(8,128)}, f32[26,128]{1,0:T(8,128)S(1)}, u32[]{:S(2)}, u32[]{:S(2)}) collective-permute-start(f32[26,128]{1,0:T(8,128)} %get-tuple-element.19), channel_id=1, source_target_pairs={{0,1},{1,0},{2,3},{3,2},{4,5},{5,4},{6,7},{7,6},{8,9},{9,8},{10,11... | collective-permute-start | bytes 39944 | tf_op jit(solution)/shard_map/ppermute | solution.py:407
  10.5 1.9 %collective-permute-start.3 = (f32[26,128]{1,0:T(8,128)}, f32[26,128]{1,0:T(8,128)S(1)}, u32[]{:S(2)}, u32[]{:S(2)}) collective-permute-start(f32[26,128]{1,0:T(8,128)} %get-tuple-element.20), channel_id=1, source_target_pairs={{0,4},{1,2},{2,1},{3,7},{4,0},{5,6},{6,5},{7,3},{8,12},{9,10},{10,... | collective-permute-start | bytes 39944 | tf_op jit(solution)/shard_map/ppermute | solution.py:407
  12.4 0.6 %copy-start.5 = (f32[26,128]{1,0:T(8,128)}, f32[26,128]{1,0:T(8,128)S(1)}, u32[]{:S(2)}) copy-start(f32[26,128]{1,0:T(8,128)S(1)} %collective-permute-done.2.got_c) | copy-start | bytes 39940
  12.4 0.6 %copy-start.6 = (f32[26,128]{1,0:T(8,128)}, f32[26,128]{1,0:T(8,128)S(1)}, u32[]{:S(2)}) copy-start(f32[26,128]{1,0:T(8,128)S(1)} %collective-permute-done.3.got_d) | copy-start | bytes 39940
  16.9 6.0 %collective-permute-start.4 = (f32[26,128]{1,0:T(8,128)}, f32[26,128]{1,0:T(8,128)S(1)}, u32[]{:S(2)}, u32[]{:S(2)}) collective-permute-start(f32[26,128]{1,0:T(8,128)} %get-tuple-element.21), channel_id=1, source_target_pairs={{0,3},{1,2},{2,1},{3,0},{4,7},{5,6},{6,5},{7,4},{8,11},{9,10},{10,... | collective-permute-start | bytes 39944 | tf_op jit(solution)/shard_map/ppermute | solution.py:407
  21.0 3.9 %collective-permute-start.5 = (f32[26,128]{1,0:T(8,128)}, f32[26,128]{1,0:T(8,128)S(1)}, u32[]{:S(2)}, u32[]{:S(2)}) collective-permute-start(f32[26,128]{1,0:T(8,128)} %get-tuple-element.22), channel_id=1, source_target_pairs={{0,1},{1,0},{2,3},{3,2},{4,5},{5,4},{6,7},{7,6},{8,9},{9,8},{10,11... | collective-permute-start | bytes 39944 | tf_op jit(solution)/shard_map/ppermute | solution.py:407
  22.1 4.8 %collective-permute-start.6 = (f32[26,128]{1,0:T(8,128)}, f32[26,128]{1,0:T(8,128)S(1)}, u32[]{:S(2)}, u32[]{:S(2)}) collective-permute-start(f32[26,128]{1,0:T(8,128)} %get-tuple-element.23), channel_id=1, source_target_pairs={{0,2},{1,3},{2,0},{3,1},{4,6},{5,7},{6,4},{7,5},{8,10},{9,11},{10,... | collective-permute-start | bytes 39944 | tf_op jit(solution)/shard_map/ppermute | solution.py:407
  22.9 4.0 %copy-start.2 = (f32[26,128]{1,0:T(8,128)}, f32[26,128]{1,0:T(8,128)S(1)}, u32[]{:S(2)}) copy-start(f32[26,128]{1,0:T(8,128)S(1)} %collective-permute-done.4.refs_0_) | copy-start | bytes 39940
  24.9 2.0 %copy-start.3 = (f32[26,128]{1,0:T(8,128)}, f32[26,128]{1,0:T(8,128)S(1)}, u32[]{:S(2)}) copy-start(f32[26,128]{1,0:T(8,128)S(1)} %collective-permute-done.5.refs_1_) | copy-start | bytes 39940
  27.0 0.6 %copy-start.4 = (f32[26,128]{1,0:T(8,128)}, f32[26,128]{1,0:T(8,128)S(1)}, u32[]{:S(2)}) copy-start(f32[26,128]{1,0:T(8,128)S(1)} %collective-permute-done.6.refs_2_) | copy-start | bytes 39940

commit v2 on v1

--- a/solution.py
+++ b/solution.py
@@ -22,10 +22,11 @@
 force_scale = 9648.53 / 28.0855
 far_away = 1.0e6
 half_pi = 1.5707963267948966
+VMEM_BYTES = 8 * 2**20
 ROWS = 8
 
 VMEM = pltpu.MemorySpace.VMEM
-SMEM = pltpu.MemorySpace.SMEM
+HBM = pltpu.MemorySpace.HBM
 
 
 def line_partner(place, count, odd):
@@ -68,17 +69,30 @@
     return pairs
 
 
-def prepare_kernel(disp, vel, force, heights, counts, lists, plan, rows, send_a, send_b, *, capacity):
+def prepare_kernel(*refs, capacity):
+    count = 7
+    sources, (rows, send_a, send_b) = refs[:count], refs[count : count + 3]
+    held, done = refs[count + 3 : -1], refs[-1]
+    copies = [
+        pltpu.make_async_copy(source, target, done.at[n])
+        for n, (source, target) in enumerate(zip(sources, held))
+    ]
+    for copy in copies:
+        copy.start()
+    disp, vel, force, heights, counts, lists, plan = held
     _, cells_x, cells_y, slots = disp.shape
     entries = lists.shape[0]
     at_x, at_y = lax.axis_index("gx"), lax.axis_index("gy")
     even_x = lax.rem(at_x, 2) == 0
+    for copy in copies:
+        copy.wait()
+    owners = [plan[:, c : c + 1] for c in range(cells_x * cells_y)]
     for x in range(cells_x):
         base_x = ((at_x * cells_x + x).astype(jnp.float32) + 0.5) * spacing
         for y in range(cells_y):
             base_y = ((at_y * cells_y + y).astype(jnp.float32) + 0.5) * spacing
             layer = heights[x, pl.ds(y, 1), :]
-            occupied = (layer < counts[x, y]).astype(jnp.float32)
+            occupied = (layer < counts[x : x + 1, y : y + 1]).astype(jnp.float32)
             lattice = (base_x, base_y, (layer.astype(jnp.float32) + 0.5) * spacing)
             column = (x * cells_y + y) * ROWS
             for q in range(3):
@@ -92,12 +106,10 @@
                 send_a[pl.ds(place, 1), :] = point
                 send_b[pl.ds(place, 1), :] = point
             rows[pl.ds(column + 6, 1), :] = occupied
-            owner = plan[x * cells_y + y]
-            earlier = 0
-            for c in range(x * cells_y + y):
-                earlier = earlier + (plan[c] == owner).astype(jnp.int32)
-            rows[pl.ds(column + 7, 1), :] = jnp.full(
-                (1, slots), (owner * capacity + earlier).astype(jnp.float32)
+            owner = owners[x * cells_y + y]
+            earlier = sum((owners[c] == owner).astype(jnp.int32) for c in range(x * cells_y + y))
+            rows[pl.ds(column + 7, 1), :] = jnp.broadcast_to(
+                (owner * capacity + earlier).astype(jnp.float32), (1, slots)
             )
             place = (3 * cells_y + y) * cells_x + x
             send_a[pl.ds(place, 1), :] = occupied
@@ -218,7 +230,7 @@
 
 
 def force_kernel(
-    rows, middle, got_a, got_b, got_c, got_d, lists, plan, *refs, counts, cells_x, cells_y, capacity, turns
+    rows, middle, got_a, got_b, got_c, got_d, lists, *refs, counts, cells_x, cells_y, capacity, turns
 ):
     outs = refs[: len(turns) + 1] if turns else refs[:1]
     table, index, parts, hot, left_side, main, ghost = refs[len(outs) :]
@@ -321,7 +333,6 @@
     line = lax.broadcasted_iota(jnp.int32, (ROWS, slots), 0)
     kick = half_step * force_scale
     chosen = (line >= 3) & (line < 6)
-    main[...] = jnp.zeros_like(main)
     for x in range(cells_x):
         for y in range(-1, cells_y + 1):
             block = reached[x, y]
@@ -330,20 +341,25 @@
                 block = parts[entries, :, y * near + x + 1, :] - block
                 column = rows[pl.ds((x * cells_y + y) * ROWS, ROWS), :]
                 column = column + jnp.where(chosen, kick * block, 0.0)
-                owner = plan[x * cells_y + y]
-                earlier = 0
-                for c in range(x * cells_y + y):
-                    earlier = earlier + (plan[c] == owner).astype(jnp.int32)
-                main[owner, pl.ds(earlier * 7, 7), :] = column[:7]
+                main[x * cells_y + y] = column
             else:
                 ghost[0 if y < 0 else 1, x] = -kick * block
     places = [4 * wide + x for x in range(cells_x)]
     below = [jnp.where(even_y, got_d[pl.ds(p, 1), :], got_c[pl.ds(p, 1), :]) for p in places]
     above = [jnp.where(even_y, got_c[pl.ds(p, 1), :], got_d[pl.ds(p, 1), :]) for p in places]
-    size = main.shape[1]
+    columns = [main[c] for c in range(cells_x * cells_y)]
+    named_here = [
+        jnp.broadcast_to(main[c, pl.ds(7, 1), :], (ROWS, slots)) for c in range(cells_x * cells_y)
+    ]
 
     def message(owner):
-        pieces = [main[owner]]
+        pieces = []
+        for slot in range(capacity):
+            wanted = (owner * capacity + slot).astype(jnp.float32)
+            piece = 0.0
+            for column, named in zip(columns, named_here):
+                piece = piece + jnp.where(named == wanted, column, 0.0)
+            pieces.append(piece[:7])
         for side, named in enumerate((below, above)):
             for slot in range(capacity):
                 wanted = (owner * capacity + slot).astype(jnp.float32)
@@ -386,9 +402,9 @@
                 speed = speed + held[source + 1, pl.ds(first + slot * 3, 3), :]
             if source > 0:
                 speed = speed + held[source - 1, pl.ds(first + (capacity + slot) * 3, 3), :]
-            out[source, slot, pl.ds(0, 3), :] = block[:3]
-            out[source, slot, pl.ds(3, 3), :] = speed
-            out[source, slot, pl.ds(6, 1), :] = block[6:7]
+            for line in range(7):
+                value = speed[line - 3 : line - 2] if 3 <= line < 6 else block[line : line + 1]
+                out[source, line, pl.ds(slot, 1), :] = value
 
 
 def per_device(displacement, velocity, forces, heights, counts, neighbours, plan):
@@ -397,8 +413,8 @@
     sizes = (lax.axis_size("gx"), lax.axis_size("gy"))
     columns = cells_x * cells_y
     capacity = max(2, (2 * columns + sizes[1] - 1) // sizes[1])
-    owners = plan.reshape(columns)
-    whole, scalar = pl.BlockSpec(memory_space=VMEM), pl.BlockSpec(memory_space=SMEM)
+    inputs = (displacement, velocity, forces, heights, counts, neighbours, plan.reshape(1, columns))
+    whole = pl.BlockSpec(memory_space=VMEM)
     shape = lambda *dims: jax.ShapeDtypeStruct(dims, jnp.float32)
     wide, near = cells_x + 4, cells_x + 2
     centers = near * cells_y
@@ -410,10 +426,13 @@
     rows, send_a, send_b = pl.pallas_call(
         functools.partial(prepare_kernel, capacity=capacity),
         out_shape=(shape(columns * ROWS, slots), shape(first_size, slots), shape(first_size, slots)),
-        in_specs=[whole, whole, whole, whole, scalar, whole, scalar],
+        in_specs=[pl.BlockSpec(memory_space=HBM)] * len(inputs),
         out_specs=(whole, whole, whole),
+        scratch_shapes=[pltpu.VMEM(value.shape, value.dtype) for value in inputs]
+        + [pltpu.SemaphoreType.DMA((len(inputs),))],
+        compiler_params=pltpu.CompilerParams(vmem_limit_bytes=VMEM_BYTES),
         name="prepare",
-    )(displacement, velocity, forces, heights, counts, neighbours, owners)
+    )(*[pltpu.with_memory_space_constraint(value, HBM) for value in inputs])
     got_a = swap(send_a, exchange_pairs(sizes, 0, False))
     got_b = swap(send_b, exchange_pairs(sizes, 0, True))
     second_size = 4 * wide + cells_x
@@ -422,6 +441,7 @@
         out_shape=(shape(4, cells_y, wide, slots), shape(second_size, slots), shape(second_size, slots)),
         in_specs=[whole] * 4,
         out_specs=(whole, whole, whole),
+        compiler_params=pltpu.CompilerParams(vmem_limit_bytes=VMEM_BYTES),
         name="strips",
     )(rows, send_a, got_a, got_b)
     got_c = swap(send_c, exchange_pairs(sizes, 1, False))
@@ -434,7 +454,7 @@
             force_kernel, counts=sizes, cells_x=cells_x, cells_y=cells_y, capacity=capacity, turns=turns
         ),
         out_shape=out_shape,
-        in_specs=[whole] * 7 + [scalar],
+        in_specs=[whole] * 7,
         out_specs=tuple(whole for _ in out_shape),
         scratch_shapes=[
             pltpu.VMEM((4, 3, near * (cells_y + 2), slots), jnp.float32),
@@ -442,11 +462,12 @@
             pltpu.VMEM((entries + 1, ROWS, centers, slots), jnp.float32),
             pltpu.VMEM((slots, entries * slots), jnp.bfloat16),
             pltpu.VMEM((9 * ROWS, entries * slots), jnp.bfloat16),
-            pltpu.VMEM((sizes[1], capacity * 7, slots), jnp.float32),
+            pltpu.VMEM((columns, ROWS, slots), jnp.float32),
             pltpu.VMEM((2, cells_x, ROWS, slots), jnp.float32),
         ],
+        compiler_params=pltpu.CompilerParams(vmem_limit_bytes=VMEM_BYTES),
         name="forces",
-    )(rows, middle, got_a, got_b, got_c, got_d, neighbours, owners)
+    )(rows, middle, got_a, got_b, got_c, got_d, neighbours)
     if turns:
         arrived = [swap(value, round_pairs(sizes, turn)) for value, turn in zip(sent, turns)]
         arrived.append(sent[-1])
@@ -456,13 +477,14 @@
         scratch = []
     result = pl.pallas_call(
         functools.partial(gather_kernel, count=sizes[1], capacity=capacity, turns=turns),
-        out_shape=shape(sizes[1], capacity, 7, slots),
+        out_shape=shape(sizes[1], 7, capacity, slots),
         in_specs=[whole] * len(arrived),
         out_specs=whole,
         scratch_shapes=scratch,
+        compiler_params=pltpu.CompilerParams(vmem_limit_bytes=VMEM_BYTES),
         name="collect",
     )(*arrived)
-    return result[None, None]
+    return jnp.swapaxes(result, 1, 2)[None, None]
 
 
 def solution(mesh):

time: 30.8 us -> 23 us (0.75)
  Pallas kernels: 8.18 us -> 4.23 us
  local copies, waits for them, and re-layouts: 3.2 us -> 0.01 us
  waiting for transfers between devices: 8.66 us -> 8.04 us
    unnamed x14 -> x2, local copies, waits for them, and re-layouts: 1.82 us -> 0.01 us
    pallas_call x1, Pallas kernels: 3.89 us -> 2.4 us  [per_device(): pl.pallas_call(functools.partial(force_kernel, counts=sizes, cells_x=cell...]
    broadcast_in_dim x1 -> x0, local copies, waits for them, and re-layouts: 1.38 us -> none  [per_device(): return result[None, None]]
    pallas_call x1, Pallas kernels: 1.4 us -> 0.03 us  [per_device(): pl.pallas_call(functools.partial(strip_kernel, count_x=sizes[0], cells_x=...]
    pallas_call x1, Pallas kernels: 1.4 us -> 0.64 us  [per_device(): pl.pallas_call(functools.partial(gather_kernel, count=sizes[1], capacity=...]
    ppermute x7, waiting for transfers between devices: 8.66 us -> 8.04 us  [swap(): return lax.ppermute(value, ('gx', 'gy'), pairs)]
    pallas_call x1, Pallas kernels: 1.49 us -> 1.16 us  [per_device(): pl.pallas_call(functools.partial(prepare_kernel, capacity=capacity), out_...]
where the time goes in v2:
time: 23 us; the launch traced here: 22.8 us
  starting transfers between devices  10.5 us (46%)
  waiting for transfers between devices  8.04 us (35%)
  Pallas kernels  4.23 us (18%)
    ppermute x7, starting transfers between devices, swap(): return lax.ppermute(value, ('gx', 'gy'), pairs)  10.5 us
    ppermute x7, waiting for transfers between devices, swap(): return lax.ppermute(value, ('gx', 'gy'), pairs)  8.04 us
    pallas_call x1, Pallas kernels, per_device(): pl.pallas_call(functools.partial(force_kernel, counts=sizes, cells_x=cell...  2.4 us
    pallas_call x1, Pallas kernels, per_device(): pl.pallas_call(functools.partial(prepare_kernel, capacity=capacity), out_...  1.16 us
    pallas_call x1, Pallas kernels, per_device(): pl.pallas_call(functools.partial(gather_kernel, count=sizes[1], capacity=...  0.64 us
  transfers between devices with their start and end apart: 7, of which 5 were waited for; matrix products, arithmetic and copies ran while one was open for 0% of the time, Pallas kernels for 0%

profile of v2, /device:TPU:0, one launch (start us, length us, event | category | flops | bytes accessed | tf_op | source)
XLA Modules:
  0.0 22.8 jit_solution(2015091017777510161)
XLA Ops:
  0.0 1.2 %prepare.1 = (f32[32,128]{1,0:T(8,128)S(1)}, f32[32,128]{1,0:T(8,128)S(1)}, f32[32,128]{1,0:T(8,128)S(1)}) custom-call(f32[3,2,2,128]{3,2,1,0:T(2,128)} %refs_0_.1, f32[3,2,2,128]{3,2,1,0:T(2,128)} %refs_1_.1, f32[3,2,2,128]{3,2,1,0:T(2,128)} %refs_2_.1, s32[2,2,128]{2,1,0:T(2,128)} %refs_3_.1, s32[2,2]{1,0:T(2,128)} %refs_4_.1, s32[8,2,2,128]{3,2,1,0:T(2,128)} %lists.1, ...), custom_call_target="tpu_custom_call" | custom-call | tf_op jit(solution)/shard_map/prepare/pallas_call | solution.py:426
  1.2 3.1 %collective-permute-start.1 = (f32[32,128]{1,0:T(8,128)S(1)}, f32[32,128]{1,0:T(8,128)S(1)}, u32[]{:S(2)}, u32[]{:S(2)}) collective-permute-start(f32[32,128]{1,0:T(8,128)S(1)} %get-tuple-element.17), channel_id=1, source_target_pairs={{0,1},{1,0},{2,3},{3,2},{4,8},{5,9},{6,10},{7,11},{8,4},{9,5},{10,... | collective-permute-start | bytes 49160 | tf_op jit(solution)/shard_map/ppermute | solution.py:423
  4.3 0.0 collective-permute-start
  4.3 1.7 %collective-permute-done.1.got_b = f32[32,128]{1,0:T(8,128)S(1)} collective-permute-done((f32[32,128]{1,0:T(8,128)S(1)}, f32[32,128]{1,0:T(8,128)S(1)}, u32[]{:S(2)}, u32[]{:S(2)}) %collective-permute-start.1) | collective-permute-done | bytes 16416 | tf_op jit(solution)/shard_map/ppermute | solution.py:423
  6.0 0.0 collective-permute-done.got_a
  6.0 0.0 copy-start
  6.0 2.1 %collective-permute-start.2 = (f32[26,128]{1,0:T(8,128)S(1)}, f32[26,128]{1,0:T(8,128)S(1)}, u32[]{:S(2)}, u32[]{:S(2)}) collective-permute-start(f32[26,128]{1,0:T(8,128)S(1)} %get-tuple-element.19), channel_id=1, source_target_pairs={{0,1},{1,0},{2,3},{3,2},{4,5},{5,4},{6,7},{7,6},{8,9},{9,8},{10,11... | collective-permute-start | bytes 39944 | tf_op jit(solution)/shard_map/ppermute | solution.py:423
  8.1 0.0 collective-permute-start.3
  8.1 1.7 %collective-permute-done.2.got_c = f32[26,128]{1,0:T(8,128)S(1)} collective-permute-done((f32[26,128]{1,0:T(8,128)S(1)}, f32[26,128]{1,0:T(8,128)S(1)}, u32[]{:S(2)}, u32[]{:S(2)}) %collective-permute-start.2) | collective-permute-done | bytes 13344 | tf_op jit(solution)/shard_map/ppermute | solution.py:423
  9.8 0.0 collective-permute-done.3.got_d
  9.9 0.0 copy-done
  9.9 2.4 %forces.1 = (f32[26,128]{1,0:T(8,128)S(1)}, f32[26,128]{1,0:T(8,128)S(1)}, f32[26,128]{1,0:T(8,128)S(1)}, f32[26,128]{1,0:T(8,128)S(1)}) custom-call(f32[32,128]{1,0:T(8,128)S(1)} %get-tuple-element.15.rows, f32[4,2,6,128]{3,2,1,0:T(8,128)S(1)} %get-tuple-element.18.middle, f32[32,128]{1,0:T(8,128)S(1)} %collective-permute-done.got_a, ...), custom_call_target="tpu_custom_call" | custom-call | tf_op jit(solution)/shard_map/forces/pallas_call | solution.py:452
  12.3 4.1 %collective-permute-start.4 = (f32[26,128]{1,0:T(8,128)S(1)}, f32[26,128]{1,0:T(8,128)S(1)}, u32[]{:S(2)}, u32[]{:S(2)}) collective-permute-start(f32[26,128]{1,0:T(8,128)S(1)} %get-tuple-element.21), channel_id=1, source_target_pairs={{0,3},{1,2},{2,1},{3,0},{4,7},{5,6},{6,5},{7,4},{8,11},{9,10},{10,... | collective-permute-start | bytes 39944 | tf_op jit(solution)/shard_map/ppermute | solution.py:423
  16.4 1.1 %collective-permute-start.5 = (f32[26,128]{1,0:T(8,128)S(1)}, f32[26,128]{1,0:T(8,128)S(1)}, u32[]{:S(2)}, u32[]{:S(2)}) collective-permute-start(f32[26,128]{1,0:T(8,128)S(1)} %get-tuple-element.22), channel_id=1, source_target_pairs={{0,1},{1,0},{2,3},{3,2},{4,5},{5,4},{6,7},{7,6},{8,9},{9,8},{10,11... | collective-permute-start | bytes 39944 | tf_op jit(solution)/shard_map/ppermute | solution.py:423
  17.5 0.0 collective-permute-start.6
  17.5 0.6 %collective-permute-done.4.refs_0_ = f32[26,128]{1,0:T(8,128)S(1)} collective-permute-done((f32[26,128]{1,0:T(8,128)S(1)}, f32[26,128]{1,0:T(8,128)S(1)}, u32[]{:S(2)}, u32[]{:S(2)}) %collective-permute-start.4) | collective-permute-done | bytes 13344 | tf_op jit(solution)/shard_map/ppermute | solution.py:423
  18.1 2.0 %collective-permute-done.5.refs_1_ = f32[26,128]{1,0:T(8,128)S(1)} collective-permute-done((f32[26,128]{1,0:T(8,128)S(1)}, f32[26,128]{1,0:T(8,128)S(1)}, u32[]{:S(2)}, u32[]{:S(2)}) %collective-permute-start.5) | collective-permute-done | bytes 13344 | tf_op jit(solution)/shard_map/ppermute | solution.py:423
  20.1 2.0 %collective-permute-done.6.refs_2_ = f32[26,128]{1,0:T(8,128)S(1)} collective-permute-done((f32[26,128]{1,0:T(8,128)S(1)}, f32[26,128]{1,0:T(8,128)S(1)}, u32[]{:S(2)}, u32[]{:S(2)}) %collective-permute-start.6) | collective-permute-done | bytes 13344 | tf_op jit(solution)/shard_map/ppermute | solution.py:423
  22.1 0.6 %collect.1 = f32[4,7,2,128]{3,2,1,0:T(2,128)} custom-call(f32[26,128]{1,0:T(8,128)S(1)} %collective-permute-done.4.refs_0_, f32[26,128]{1,0:T(8,128)S(1)} %collective-permute-done.5.refs_1_, f32[26,128]{1,0:T(8,128)S(1)} %collective-permute-done.6.refs_2_, f32[26,128]{1,0:T(8,128)S(1)} %get-tuple-element.24.refs_3_), custom_call_target="tpu_custom_call" | custom-call | tf_op jit(solution)/shard_map/collect/pallas_call | solution.py:478
  (1 shorter events, 0.0 us)
Async XLA Ops:
  1.2 4.8 %collective-permute-start.1 = (f32[32,128]{1,0:T(8,128)S(1)}, f32[32,128]{1,0:T(8,128)S(1)}, u32[]{:S(2)}, u32[]{:S(2)}) collective-permute-start(f32[32,128]{1,0:T(8,128)S(1)} %get-tuple-element.17), channel_id=1, source_target_pairs={{0,1},{1,0},{2,3},{3,2},{4,8},{5,9},{6,10},{7,11},{8,4},{9,5},{10,... | collective-permute-start | bytes 49160 | tf_op jit(solution)/shard_map/ppermute | solution.py:423
  4.3 1.7 %collective-permute-start = (f32[32,128]{1,0:T(8,128)S(1)}, f32[32,128]{1,0:T(8,128)S(1)}, u32[]{:S(2)}, u32[]{:S(2)}) collective-permute-start(f32[32,128]{1,0:T(8,128)S(1)} %get-tuple-element.16.own), channel_id=1, source_target_pairs={{0,4},{1,5},{2,6},{3,7},{4,0},{5,1},{6,2},{7,3},{8,12},{9,13},{10,... | collective-permute-start | bytes 49160 | tf_op jit(solution)/shard_map/ppermute | solution.py:423
  6.0 3.8 %copy-start = (s32[8,2,2,128]{3,2,1,0:T(2,128)S(1)}, s32[8,2,2,128]{3,2,1,0:T(2,128)}, u32[]{:S(2)}) copy-start(s32[8,2,2,128]{3,2,1,0:T(2,128)} %lists.1) | copy-start | bytes 49156
  6.0 3.8 %collective-permute-start.2 = (f32[26,128]{1,0:T(8,128)S(1)}, f32[26,128]{1,0:T(8,128)S(1)}, u32[]{:S(2)}, u32[]{:S(2)}) collective-permute-start(f32[26,128]{1,0:T(8,128)S(1)} %get-tuple-element.19), channel_id=1, source_target_pairs={{0,1},{1,0},{2,3},{3,2},{4,5},{5,4},{6,7},{7,6},{8,9},{9,8},{10,11... | collective-permute-start | bytes 39944 | tf_op jit(solution)/shard_map/ppermute | solution.py:423
  8.1 1.7 %collective-permute-start.3 = (f32[26,128]{1,0:T(8,128)S(1)}, f32[26,128]{1,0:T(8,128)S(1)}, u32[]{:S(2)}, u32[]{:S(2)}) collective-permute-start(f32[26,128]{1,0:T(8,128)S(1)} %get-tuple-element.20), channel_id=1, source_target_pairs={{0,4},{1,2},{2,1},{3,7},{4,0},{5,6},{6,5},{7,3},{8,12},{9,10},{10,... | collective-permute-start | bytes 39944 | tf_op jit(solution)/shard_map/ppermute | solution.py:423
  12.3 5.8 %collective-permute-start.4 = (f32[26,128]{1,0:T(8,128)S(1)}, f32[26,128]{1,0:T(8,128)S(1)}, u32[]{:S(2)}, u32[]{:S(2)}) collective-permute-start(f32[26,128]{1,0:T(8,128)S(1)} %get-tuple-element.21), channel_id=1, source_target_pairs={{0,3},{1,2},{2,1},{3,0},{4,7},{5,6},{6,5},{7,4},{8,11},{9,10},{10,... | collective-permute-start | bytes 39944 | tf_op jit(solution)/shard_map/ppermute | solution.py:423
  16.4 3.7 %collective-permute-start.5 = (f32[26,128]{1,0:T(8,128)S(1)}, f32[26,128]{1,0:T(8,128)S(1)}, u32[]{:S(2)}, u32[]{:S(2)}) collective-permute-start(f32[26,128]{1,0:T(8,128)S(1)} %get-tuple-element.22), channel_id=1, source_target_pairs={{0,1},{1,0},{2,3},{3,2},{4,5},{5,4},{6,7},{7,6},{8,9},{9,8},{10,11... | collective-permute-start | bytes 39944 | tf_op jit(solution)/shard_map/ppermute | solution.py:423
  17.5 4.6 %collective-permute-start.6 = (f32[26,128]{1,0:T(8,128)S(1)}, f32[26,128]{1,0:T(8,128)S(1)}, u32[]{:S(2)}, u32[]{:S(2)}) collective-permute-start(f32[26,128]{1,0:T(8,128)S(1)} %get-tuple-element.23), channel_id=1, source_target_pairs={{0,2},{1,3},{2,0},{3,1},{4,6},{5,7},{6,4},{7,5},{8,10},{9,11},{10,... | collective-permute-start | bytes 39944 | tf_op jit(solution)/shard_map/ppermute | solution.py:423

commit v3 on v2

--- a/solution.py
+++ b/solution.py
@@ -229,16 +229,13 @@
     return grads
 
 
-def force_kernel(
-    rows, middle, got_a, got_b, got_c, got_d, lists, *refs, counts, cells_x, cells_y, capacity, turns
+def near_kernel(
+    middle, got_a, got_b, lists, centre, nearby, slot_at, cell_at, spots, cells, table, index, *, cells_x, cells_y
 ):
-    outs = refs[: len(turns) + 1] if turns else refs[:1]
-    table, index, parts, hot, left_side, main, ghost = refs[len(outs) :]
     entries, slots = lists.shape[0], lists.shape[3]
     shift = slots.bit_length() - 1
-    at_x, at_y = lax.axis_index("gx"), lax.axis_index("gy")
-    even_x, even_y = lax.rem(at_x, 2) == 0, lax.rem(at_y, 2) == 0
-    wide, near = cells_x + 4, cells_x + 2
+    even_x = lax.rem(lax.axis_index("gx"), 2) == 0
+    near = cells_x + 2
     centers = near * cells_y
     base = 4 * cells_x * cells_y
     for m in range(entries):
@@ -250,79 +247,130 @@
             for x in range(cells_x):
                 index[m, pl.ds(y * near + 1 + x, 1), :] = lists[m, x, pl.ds(y, 1), :]
             index[m, pl.ds(y * near + near - 1, 1), :] = right[y : y + 1]
-    has_below, has_above = at_y > 0, at_y < counts[1] - 1
-    strips = []
-    for y in range(-1, cells_y + 1):
-        if 0 <= y < cells_y:
-            strip = [middle[q, y] for q in range(4)]
-        else:
-            swap, there = (even_y, has_below) if y < 0 else (jnp.logical_not(even_y), has_above)
-            strip = [
-                jnp.where(swap, got_d[pl.ds(q * wide, wide), :], got_c[pl.ds(q * wide, wide), :])
-                for q in range(4)
-            ]
-            strip[3] = strip[3] * there.astype(jnp.float32)
+    for y in range(cells_y):
+        strip = [middle[q, y] for q in range(4)]
+        centre[3, pl.ds(y * near, near), :] = strip[3][1 : 1 + near]
         strip[2] = jnp.where(strip[3] > 0.0, strip[2], far_away)
+        for q in range(3):
+            for move in range(3):
+                table[q, move, pl.ds((y + 1) * near, near), :] = strip[q][move : move + near]
+    for q in range(3):
         for move in range(3):
-            for q in range(4):
-                table[q, move, pl.ds((y + 1) * near, near), :] = strip[q][move : move + near]
-    center = [table[q, 1, pl.ds(near, centers), :] for q in range(4)]
-    occupied = center[3]
-    entry_slot, entry_cell = [], []
+            for y in (0, cells_y + 1):
+                table[q, move, pl.ds(y * near, near), :] = jnp.zeros((near, slots), jnp.float32)
+        centre[q] = table[q, 1, pl.ds(near, centers), :]
+    line = lax.broadcasted_iota(jnp.int32, (centers, slots), 0)
     for m in range(entries):
         value = index[m]
-        entry_slot.append(value & (slots - 1))
-        entry_cell.append(value >> shift)
-    nearby = [[None] * 3 for _ in range(entries)]
-    for q in range(3):
+        slot, cell = value & (slots - 1), value >> shift
+        picked = []
         for c in range(9):
-            source = table[q, c // 3, pl.ds((c % 3) * near, centers), :]
-            for m in range(entries):
-                picked = jnp.take_along_axis(
-                    source, entry_slot[m], axis=1, mode="promise_in_bounds"
-                )
-                nearby[m][q] = (
-                    picked if c == 0 else jnp.where(entry_cell[m] == c, picked, nearby[m][q])
-                )
-    grads = column_gradients(center[:3], occupied, nearby)
+            for q in range(3):
+                source = table[q, c // 3, pl.ds((c % 3) * near, centers), :]
+                got = jnp.take_along_axis(source, slot, axis=1, mode="promise_in_bounds")
+                if c == 0:
+                    picked.append(got)
+                else:
+                    picked[q] = jnp.where(cell == c, got, picked[q])
+        for q in range(3):
+            nearby[m, q] = picked[q]
+        move_x = jnp.where(cell < 3, 0, jnp.where(cell < 6, 1, 2))
+        move_y = cell - 3 * move_x
+        away = ((line < near) & (move_y == 0)) | ((line >= centers - near) & (move_y == 2))
+        slot_at[m] = slot
+        cell_at[m] = jnp.where(away, move_x, 3)
+        spots[pl.ds(m * centers, centers), :] = slot.astype(jnp.float32)
+        cells[pl.ds(m * centers, centers), :] = cell.astype(jnp.float32)
+
+
+def force_kernel(
+    rows, centre, nearby_own, slot_at, cell_at, spots, cells, got_c, got_d, *refs,
+    counts, cells_x, cells_y, capacity, turns
+):
+    outs = refs[: len(turns) + 1] if turns else refs[:1]
+    table, parts, main, ghost = refs[len(outs) :]
+    entries, centers, slots = slot_at.shape
+    at_y = lax.axis_index("gy")
+    even_y = lax.rem(at_y, 2) == 0
+    wide, near = cells_x + 4, cells_x + 2
+    has_below, has_above = at_y > 0, at_y < counts[1] - 1
+    for row, swap, there in (
+        (0, even_y, has_below),
+        (centers - near, jnp.logical_not(even_y), has_above),
+    ):
+        strip = [
+            jnp.where(swap, got_d[pl.ds(q * wide, wide), :], got_c[pl.ds(q * wide, wide), :])
+            for q in range(4)
+        ]
+        full = strip[3] * there.astype(jnp.float32) > 0.0
+        strip[2] = jnp.where(full, strip[2], far_away)
+        for move in range(3):
+            for q in range(3):
+                table[q, move, pl.ds(row, near), :] = strip[q][move : move + near]
+    for y in range(1, cells_y - 1):
+        for move in range(3):
+            for q in range(3):
+                table[q, move, pl.ds(y * near, near), :] = jnp.zeros((near, slots), jnp.float32)
+    center = [centre[q] for q in range(3)]
+    occupied = centre[3]
+    nearby = []
+    for m in range(entries):
+        picked = [nearby_own[m, q] for q in range(3)]
+        slot, cell = slot_at[m], cell_at[m]
+        for move in range(3):
+            for q in range(3):
+                got = jnp.take_along_axis(table[q, move], slot, axis=1, mode="promise_in_bounds")
+                picked[q] = jnp.where(cell == move, got, picked[q])
+        nearby.append(picked)
+    grads = column_gradients(center, occupied, nearby)
     own = [sum(grads[m][q] for m in range(entries)) for q in range(3)]
+    zero = jnp.zeros_like(occupied)
+
+    def part(m, row):
+        return pl.ds((m * ROWS + row) * centers, centers)
+
+    def column_parts(m, i):
+        return parts[pl.ds(m * ROWS * centers + i, ROWS, stride=centers), :]
+
     for m in range(entries):
-        index[m] = entry_slot[m]
         for q in range(3):
             high = grads[m][q].astype(jnp.bfloat16).astype(jnp.float32)
-            parts[m, 3 + q] = high
-            parts[m, q] = grads[m][q] - high
-        parts[m, 6] = entry_cell[m].astype(jnp.float32)
-        parts[m, 7] = jnp.zeros_like(occupied)
+            parts[part(m, 3 + q), :] = high
+            parts[part(m, q), :] = grads[m][q] - high
+        for row in (6, 7):
+            parts[part(m, row), :] = zero
     for q in range(3):
-        parts[entries, q] = jnp.zeros_like(occupied)
-        parts[entries, 3 + q] = own[q]
-    for q in (6, 7):
-        parts[entries, q] = jnp.zeros_like(occupied)
+        parts[part(entries, 3 + q), :] = own[q]
+    for row in (0, 1, 2, 6, 7):
+        parts[part(entries, row), :] = zero
     reached = {}
-    ramp = lax.broadcasted_iota(jnp.int32, (slots, slots), 0)
+    step = 16
+    ramps = [
+        (lax.broadcasted_iota(jnp.int32, (step, slots), 0) + first).astype(jnp.float32).astype(jnp.bfloat16)
+        for first in range(0, slots, step)
+    ]
+    one, none = jnp.ones((step, slots), jnp.bfloat16), jnp.zeros((step, slots), jnp.bfloat16)
     for y in range(cells_y):
         for x in range(-1, cells_x + 1):
             i = y * near + x + 1
             targets = [
                 (dx, dy) for dx in (-1, 0, 1) if 0 <= x + dx < cells_x for dy in (-1, 0, 1)
             ]
+            hot, left_side = [], []
             for m in range(entries):
-                lanes = pl.ds(m * slots, slots)
-                row = jnp.broadcast_to(index[m, pl.ds(i, 1), :], (slots, slots))
-                hot[:, lanes] = jnp.where(ramp == row, 1.0, 0.0).astype(jnp.bfloat16)
-                values = parts[m, :, i, :]
-                cell = jnp.broadcast_to(parts[m, 6, pl.ds(i, 1), :], (ROWS, slots))
-                masked = []
-                for dx, dy in targets:
-                    c = (dx + 1) * 3 + dy + 1
-                    masked.append(jnp.where(cell == float(c), values, 0.0))
-                left_side[pl.ds(0, ROWS * len(targets)), lanes] = jnp.concatenate(
-                    masked, axis=0
-                ).astype(jnp.bfloat16)
+                row = spots[pl.ds(m * centers + i, step, stride=0), :].astype(jnp.bfloat16)
+                hot.append(
+                    jnp.concatenate([jnp.where(ramp == row, one, none) for ramp in ramps], axis=0)
+                )
+                values = column_parts(m, i)
+                cell = cells[pl.ds(m * centers + i, ROWS, stride=0), :]
+                masked = [
+                    jnp.where(cell == float((dx + 1) * 3 + dy + 1), values, 0.0) for dx, dy in targets
+                ]
+                left_side.append(jnp.concatenate(masked, axis=0).astype(jnp.bfloat16))
             sums = lax.dot_general(
-                left_side[pl.ds(0, ROWS * len(targets)), :],
-                hot[...],
+                jnp.concatenate(left_side, axis=1),
+                jnp.concatenate(hot, axis=1),
                 (((1,), (1,)), ((), ())),
                 preferred_element_type=jnp.float32,
             )
@@ -338,7 +386,7 @@
             block = reached[x, y]
             block = block + pltpu.roll(block, 3, 0)
             if 0 <= y < cells_y:
-                block = parts[entries, :, y * near + x + 1, :] - block
+                block = column_parts(entries, y * near + x + 1) - block
                 column = rows[pl.ds((x * cells_y + y) * ROWS, ROWS), :]
                 column = column + jnp.where(chosen, kick * block, 0.0)
                 main[x * cells_y + y] = column
@@ -449,25 +497,43 @@
     turns = tuple(range(sizes[1] - 1)) if sizes[1] in (2, 4) else ()
     size = capacity * 13
     out_shape = (shape(size, slots),) * (len(turns) + 1) if turns else (shape(sizes[1], size, slots),)
+    flat = lambda kind, *dims: jax.ShapeDtypeStruct(dims, kind)
+    found = pl.pallas_call(
+        functools.partial(near_kernel, cells_x=cells_x, cells_y=cells_y),
+        out_shape=(
+            shape(4, centers, slots),
+            shape(entries, 3, centers, slots),
+            flat(jnp.int32, entries, centers, slots),
+            flat(jnp.int32, entries, centers, slots),
+            shape(entries * centers, slots),
+            shape(entries * centers, slots),
+        ),
+        in_specs=[whole] * 4,
+        out_specs=(whole,) * 6,
+        scratch_shapes=[
+            pltpu.VMEM((3, 3, near * (cells_y + 2), slots), jnp.float32),
+            pltpu.VMEM((entries, centers, slots), jnp.int32),
+        ],
+        compiler_params=pltpu.CompilerParams(vmem_limit_bytes=VMEM_BYTES),
+        cost_estimate=pl.CostEstimate(flops=1000000, bytes_accessed=200000, transcendentals=0),
+        name="near",
+    )(middle, got_a, got_b, neighbours)
     sent = pl.pallas_call(
         functools.partial(
             force_kernel, counts=sizes, cells_x=cells_x, cells_y=cells_y, capacity=capacity, turns=turns
         ),
         out_shape=out_shape,
-        in_specs=[whole] * 7,
+        in_specs=[whole] * 9,
         out_specs=tuple(whole for _ in out_shape),
         scratch_shapes=[
-            pltpu.VMEM((4, 3, near * (cells_y + 2), slots), jnp.float32),
-            pltpu.VMEM((entries, centers, slots), jnp.int32),
-            pltpu.VMEM((entries + 1, ROWS, centers, slots), jnp.float32),
-            pltpu.VMEM((slots, entries * slots), jnp.bfloat16),
-            pltpu.VMEM((9 * ROWS, entries * slots), jnp.bfloat16),
+            pltpu.VMEM((3, 3, centers, slots), jnp.float32),
+            pltpu.VMEM(((entries + 1) * ROWS * centers, slots), jnp.float32),
             pltpu.VMEM((columns, ROWS, slots), jnp.float32),
             pltpu.VMEM((2, cells_x, ROWS, slots), jnp.float32),
         ],
         compiler_params=pltpu.CompilerParams(vmem_limit_bytes=VMEM_BYTES),
         name="forces",
-    )(rows, middle, got_a, got_b, got_c, got_d, neighbours)
+    )(rows, *found, got_c, got_d)
     if turns:
         arrived = [swap(value, round_pairs(sizes, turn)) for value, turn in zip(sent, turns)]
         arrived.append(sent[-1])

time: 23 us -> 21.9 us (0.952)
  Pallas kernels: 4.23 us -> 3.49 us
  waiting for transfers between devices: 8.04 us -> 7.68 us
    pallas_call x1, Pallas kernels: 2.4 us -> 1.31 us  [per_device(): pl.pallas_call(functools.partial(force_kernel, counts=sizes, cells_x=cell...]
    ppermute x7, waiting for transfers between devices: 8.04 us -> 7.68 us  [swap(): return lax.ppermute(value, ('gx', 'gy'), pairs)]
    pallas_call x0 -> x1, Pallas kernels: none -> 0.35 us  [per_device(): pl.pallas_call(functools.partial(near_kernel, cells_x=cells_x, cells_y=ce...]
  transfers between devices with their start and end apart: 7 -> 7, of which waited for: 5 -> 5; matrix products, arithmetic and copies ran while one was open for 0% -> 0% of each run, Pallas kernels for 0% -> 2%
where the time goes in v3:
time: 21.9 us; the launch traced here: 21.7 us
  starting transfers between devices  10.5 us (48%)
  waiting for transfers between devices  7.68 us (35%)
  Pallas kernels  3.49 us (16%)
    ppermute x7, starting transfers between devices, swap(): return lax.ppermute(value, ('gx', 'gy'), pairs)  10.5 us
    ppermute x7, waiting for transfers between devices, swap(): return lax.ppermute(value, ('gx', 'gy'), pairs)  7.68 us
    pallas_call x1, Pallas kernels, per_device(): pl.pallas_call(functools.partial(force_kernel, counts=sizes, cells_x=cell...  1.31 us
    pallas_call x1, Pallas kernels, per_device(): pl.pallas_call(functools.partial(prepare_kernel, capacity=capacity), out_...  1.16 us
    pallas_call x1, Pallas kernels, per_device(): pl.pallas_call(functools.partial(gather_kernel, count=sizes[1], capacity=...  0.64 us
  transfers between devices with their start and end apart: 7, of which 5 were waited for; matrix products, arithmetic and copies ran while one was open for 0% of the time, Pallas kernels for 2%

profile of v3, /device:TPU:0, one launch (start us, length us, event | category | flops | bytes accessed | tf_op | source)
XLA Modules:
  0.0 21.7 jit_solution(7376117248935236930)
XLA Ops:
  0.0 1.2 %prepare.1 = (f32[32,128]{1,0:T(8,128)S(1)}, f32[32,128]{1,0:T(8,128)S(1)}, f32[32,128]{1,0:T(8,128)S(1)}) custom-call(f32[3,2,2,128]{3,2,1,0:T(2,128)} %refs_0_.1, f32[3,2,2,128]{3,2,1,0:T(2,128)} %refs_1_.1, f32[3,2,2,128]{3,2,1,0:T(2,128)} %refs_2_.1, s32[2,2,128]{2,1,0:T(2,128)} %refs_3_.1, s32[2,2]{1,0:T(2,128)} %refs_4_.1, s32[8,2,2,128]{3,2,1,0:T(2,128)} %lists.1, ...), custom_call_target="tpu_custom_call" | custom-call | tf_op jit(solution)/shard_map/prepare/pallas_call | solution.py:474
  1.2 3.1 %collective-permute-start.1 = (f32[32,128]{1,0:T(8,128)S(1)}, f32[32,128]{1,0:T(8,128)S(1)}, u32[]{:S(2)}, u32[]{:S(2)}) collective-permute-start(f32[32,128]{1,0:T(8,128)S(1)} %get-tuple-element.23), channel_id=1, source_target_pairs={{0,1},{1,0},{2,3},{3,2},{4,8},{5,9},{6,10},{7,11},{8,4},{9,5},{10,... | collective-permute-start | bytes 49160 | tf_op jit(solution)/shard_map/ppermute | solution.py:471
  4.3 0.0 collective-permute-start
  4.3 1.7 %collective-permute-done.1.got_b = f32[32,128]{1,0:T(8,128)S(1)} collective-permute-done((f32[32,128]{1,0:T(8,128)S(1)}, f32[32,128]{1,0:T(8,128)S(1)}, u32[]{:S(2)}, u32[]{:S(2)}) %collective-permute-start.1) | collective-permute-done | bytes 16416 | tf_op jit(solution)/shard_map/ppermute | solution.py:471
  6.0 0.0 collective-permute-done.got_a
  6.0 0.0 copy-start
  6.0 2.1 %collective-permute-start.2 = (f32[26,128]{1,0:T(8,128)S(1)}, f32[26,128]{1,0:T(8,128)S(1)}, u32[]{:S(2)}, u32[]{:S(2)}) collective-permute-start(f32[26,128]{1,0:T(8,128)S(1)} %get-tuple-element.31), channel_id=1, source_target_pairs={{0,1},{1,0},{2,3},{3,2},{4,5},{5,4},{6,7},{7,6},{8,9},{9,8},{10,11... | collective-permute-start | bytes 39944 | tf_op jit(solution)/shard_map/ppermute | solution.py:471
  8.1 0.0 collective-permute-start.3
  8.1 0.0 copy-done
  8.1 0.4 %near.1 = (f32[4,8,128]{2,1,0:T(8,128)S(1)}, f32[8,3,8,128]{3,2,1,0:T(8,128)S(1)}, s32[8,8,128]{2,1,0:T(8,128)S(1)}, s32[8,8,128]{2,1,0:T(8,128)S(1)}, f32[64,128]{1,0:T(8,128)S(1)}, /*index=5*/f32[64,128]{1,0:T(8,128)S(1)}) custom-call(f32[4,2,6,128]{3,2,1,0:T(8,128)S(1)} %get-tuple-element.24.middle, f32[32,128]{1,0:T(8,128)S(1)} %collective-permute-done.got_a, ...), custom_call_target="tpu_custom_call" | custom-call | flops 1000000 | bytes 200000 | tf_op jit(solution)/shard_map/near/pallas_call | solution.py:501
  8.5 1.4 %collective-permute-done.2.got_c = f32[26,128]{1,0:T(8,128)S(1)} collective-permute-done((f32[26,128]{1,0:T(8,128)S(1)}, f32[26,128]{1,0:T(8,128)S(1)}, u32[]{:S(2)}, u32[]{:S(2)}) %collective-permute-start.2) | collective-permute-done | bytes 13344 | tf_op jit(solution)/shard_map/ppermute | solution.py:471
  9.8 0.0 collective-permute-done.3.got_d
  9.9 1.3 %forces.1 = (f32[26,128]{1,0:T(8,128)S(1)}, f32[26,128]{1,0:T(8,128)S(1)}, f32[26,128]{1,0:T(8,128)S(1)}, f32[26,128]{1,0:T(8,128)S(1)}) custom-call(f32[32,128]{1,0:T(8,128)S(1)} %get-tuple-element.21.rows, f32[4,8,128]{2,1,0:T(8,128)S(1)} %get-tuple-element.25.centre, f32[8,3,8,128]{3,2,1,0:T(8,128)S(1)} %get-tuple-element.26.nearby_own, ...), custom_call_target="tpu_custom_call" | custom-call | tf_op jit(solution)/shard_map/forces/pallas_call | solution.py:521
  11.2 4.1 %collective-permute-start.4 = (f32[26,128]{1,0:T(8,128)S(1)}, f32[26,128]{1,0:T(8,128)S(1)}, u32[]{:S(2)}, u32[]{:S(2)}) collective-permute-start(f32[26,128]{1,0:T(8,128)S(1)} %get-tuple-element.33), channel_id=1, source_target_pairs={{0,3},{1,2},{2,1},{3,0},{4,7},{5,6},{6,5},{7,4},{8,11},{9,10},{10,... | collective-permute-start | bytes 39944 | tf_op jit(solution)/shard_map/ppermute | solution.py:471
  15.3 1.1 %collective-permute-start.5 = (f32[26,128]{1,0:T(8,128)S(1)}, f32[26,128]{1,0:T(8,128)S(1)}, u32[]{:S(2)}, u32[]{:S(2)}) collective-permute-start(f32[26,128]{1,0:T(8,128)S(1)} %get-tuple-element.34), channel_id=1, source_target_pairs={{0,1},{1,0},{2,3},{3,2},{4,5},{5,4},{6,7},{7,6},{8,9},{9,8},{10,11... | collective-permute-start | bytes 39944 | tf_op jit(solution)/shard_map/ppermute | solution.py:471
  16.4 0.0 collective-permute-start.6
  16.4 0.6 %collective-permute-done.4.refs_0_ = f32[26,128]{1,0:T(8,128)S(1)} collective-permute-done((f32[26,128]{1,0:T(8,128)S(1)}, f32[26,128]{1,0:T(8,128)S(1)}, u32[]{:S(2)}, u32[]{:S(2)}) %collective-permute-start.4) | collective-permute-done | bytes 13344 | tf_op jit(solution)/shard_map/ppermute | solution.py:471
  17.0 2.0 %collective-permute-done.5.refs_1_ = f32[26,128]{1,0:T(8,128)S(1)} collective-permute-done((f32[26,128]{1,0:T(8,128)S(1)}, f32[26,128]{1,0:T(8,128)S(1)}, u32[]{:S(2)}, u32[]{:S(2)}) %collective-permute-start.5) | collective-permute-done | bytes 13344 | tf_op jit(solution)/shard_map/ppermute | solution.py:471
  19.0 2.0 %collective-permute-done.6.refs_2_ = f32[26,128]{1,0:T(8,128)S(1)} collective-permute-done((f32[26,128]{1,0:T(8,128)S(1)}, f32[26,128]{1,0:T(8,128)S(1)}, u32[]{:S(2)}, u32[]{:S(2)}) %collective-permute-start.6) | collective-permute-done | bytes 13344 | tf_op jit(solution)/shard_map/ppermute | solution.py:471
  21.0 0.6 %collect.1 = f32[4,7,2,128]{3,2,1,0:T(2,128)} custom-call(f32[26,128]{1,0:T(8,128)S(1)} %collective-permute-done.4.refs_0_, f32[26,128]{1,0:T(8,128)S(1)} %collective-permute-done.5.refs_1_, f32[26,128]{1,0:T(8,128)S(1)} %collective-permute-done.6.refs_2_, f32[26,128]{1,0:T(8,128)S(1)} %get-tuple-element.36.refs_3_), custom_call_target="tpu_custom_call" | custom-call | tf_op jit(solution)/shard_map/collect/pallas_call | solution.py:544
  (1 shorter events, 0.0 us)
Async XLA Ops:
  1.2 4.8 %collective-permute-start.1 = (f32[32,128]{1,0:T(8,128)S(1)}, f32[32,128]{1,0:T(8,128)S(1)}, u32[]{:S(2)}, u32[]{:S(2)}) collective-permute-start(f32[32,128]{1,0:T(8,128)S(1)} %get-tuple-element.23), channel_id=1, source_target_pairs={{0,1},{1,0},{2,3},{3,2},{4,8},{5,9},{6,10},{7,11},{8,4},{9,5},{10,... | collective-permute-start | bytes 49160 | tf_op jit(solution)/shard_map/ppermute | solution.py:471
  4.3 1.7 %collective-permute-start = (f32[32,128]{1,0:T(8,128)S(1)}, f32[32,128]{1,0:T(8,128)S(1)}, u32[]{:S(2)}, u32[]{:S(2)}) collective-permute-start(f32[32,128]{1,0:T(8,128)S(1)} %get-tuple-element.22.own), channel_id=1, source_target_pairs={{0,4},{1,5},{2,6},{3,7},{4,0},{5,1},{6,2},{7,3},{8,12},{9,13},{10,... | collective-permute-start | bytes 49160 | tf_op jit(solution)/shard_map/ppermute | solution.py:471
  6.0 2.1 %copy-start = (s32[8,2,2,128]{3,2,1,0:T(2,128)S(1)}, s32[8,2,2,128]{3,2,1,0:T(2,128)}, u32[]{:S(2)}) copy-start(s32[8,2,2,128]{3,2,1,0:T(2,128)} %lists.1) | copy-start | bytes 49156
  6.0 3.8 %collective-permute-start.2 = (f32[26,128]{1,0:T(8,128)S(1)}, f32[26,128]{1,0:T(8,128)S(1)}, u32[]{:S(2)}, u32[]{:S(2)}) collective-permute-start(f32[26,128]{1,0:T(8,128)S(1)} %get-tuple-element.31), channel_id=1, source_target_pairs={{0,1},{1,0},{2,3},{3,2},{4,5},{5,4},{6,7},{7,6},{8,9},{9,8},{10,11... | collective-permute-start | bytes 39944 | tf_op jit(solution)/shard_map/ppermute | solution.py:471
  8.1 1.7 %collective-permute-start.3 = (f32[26,128]{1,0:T(8,128)S(1)}, f32[26,128]{1,0:T(8,128)S(1)}, u32[]{:S(2)}, u32[]{:S(2)}) collective-permute-start(f32[26,128]{1,0:T(8,128)S(1)} %get-tuple-element.32), channel_id=1, source_target_pairs={{0,4},{1,2},{2,1},{3,7},{4,0},{5,6},{6,5},{7,3},{8,12},{9,10},{10,... | collective-permute-start | bytes 39944 | tf_op jit(solution)/shard_map/ppermute | solution.py:471
  11.2 5.8 %collective-permute-start.4 = (f32[26,128]{1,0:T(8,128)S(1)}, f32[26,128]{1,0:T(8,128)S(1)}, u32[]{:S(2)}, u32[]{:S(2)}) collective-permute-start(f32[26,128]{1,0:T(8,128)S(1)} %get-tuple-element.33), channel_id=1, source_target_pairs={{0,3},{1,2},{2,1},{3,0},{4,7},{5,6},{6,5},{7,4},{8,11},{9,10},{10,... | collective-permute-start | bytes 39944 | tf_op jit(solution)/shard_map/ppermute | solution.py:471
  15.3 3.7 %collective-permute-start.5 = (f32[26,128]{1,0:T(8,128)S(1)}, f32[26,128]{1,0:T(8,128)S(1)}, u32[]{:S(2)}, u32[]{:S(2)}) collective-permute-start(f32[26,128]{1,0:T(8,128)S(1)} %get-tuple-element.34), channel_id=1, source_target_pairs={{0,1},{1,0},{2,3},{3,2},{4,5},{5,4},{6,7},{7,6},{8,9},{9,8},{10,11... | collective-permute-start | bytes 39944 | tf_op jit(solution)/shard_map/ppermute | solution.py:471
  16.4 4.6 %collective-permute-start.6 = (f32[26,128]{1,0:T(8,128)S(1)}, f32[26,128]{1,0:T(8,128)S(1)}, u32[]{:S(2)}, u32[]{:S(2)}) collective-permute-start(f32[26,128]{1,0:T(8,128)S(1)} %get-tuple-element.35), channel_id=1, source_target_pairs={{0,2},{1,3},{2,0},{3,1},{4,6},{5,7},{6,4},{7,5},{8,10},{9,11},{10,... | collective-permute-start | bytes 39944 | tf_op jit(solution)/shard_map/ppermute | solution.py:471

commit v4 on v3

--- a/solution.py
+++ b/solution.py
@@ -343,20 +343,18 @@
         parts[part(entries, 3 + q), :] = own[q]
     for row in (0, 1, 2, 6, 7):
         parts[part(entries, row), :] = zero
-    reached = {}
     step = 16
     ramps = [
         (lax.broadcasted_iota(jnp.int32, (step, slots), 0) + first).astype(jnp.float32).astype(jnp.bfloat16)
         for first in range(0, slots, step)
     ]
     one, none = jnp.ones((step, slots), jnp.bfloat16), jnp.zeros((step, slots), jnp.bfloat16)
+    targets = [(x, y) for x in range(cells_x) for y in range(-1, cells_y + 1)]
+    empty = jnp.zeros((ROWS, slots), jnp.float32)
+    hot, values_at = [], []
     for y in range(cells_y):
         for x in range(-1, cells_x + 1):
             i = y * near + x + 1
-            targets = [
-                (dx, dy) for dx in (-1, 0, 1) if 0 <= x + dx < cells_x for dy in (-1, 0, 1)
-            ]
-            hot, left_side = [], []
             for m in range(entries):
                 row = spots[pl.ds(m * centers + i, step, stride=0), :].astype(jnp.bfloat16)
                 hot.append(
@@ -364,20 +362,20 @@
                 )
                 values = column_parts(m, i)
                 cell = cells[pl.ds(m * centers + i, ROWS, stride=0), :]
-                masked = [
-                    jnp.where(cell == float((dx + 1) * 3 + dy + 1), values, 0.0) for dx, dy in targets
-                ]
-                left_side.append(jnp.concatenate(masked, axis=0).astype(jnp.bfloat16))
-            sums = lax.dot_general(
-                jnp.concatenate(left_side, axis=1),
-                jnp.concatenate(hot, axis=1),
-                (((1,), (1,)), ((), ())),
-                preferred_element_type=jnp.float32,
-            )
-            for n, (dx, dy) in enumerate(targets):
-                key = (x + dx, y + dy)
-                block = sums[n * ROWS : (n + 1) * ROWS]
-                reached[key] = block if key not in reached else reached[key] + block
+                masked = []
+                for to_x, to_y in targets:
+                    dx, dy = to_x - x, to_y - y
+                    near_by = -1 <= dx <= 1 and -1 <= dy <= 1
+                    c = float((dx + 1) * 3 + dy + 1)
+                    masked.append(jnp.where(cell == c, values, 0.0) if near_by else empty)
+                values_at.append(jnp.concatenate(masked, axis=0).astype(jnp.bfloat16))
+    sums = jnp.transpose(lax.dot_general(
+        jnp.concatenate(hot, axis=1),
+        jnp.concatenate(values_at, axis=1),
+        (((1,), (1,)), ((), ())),
+        preferred_element_type=jnp.float32,
+    ))
+    reached = {key: sums[n * ROWS : (n + 1) * ROWS] for n, key in enumerate(targets)}
     line = lax.broadcasted_iota(jnp.int32, (ROWS, slots), 0)
     kick = half_step * force_scale
     chosen = (line >= 3) & (line < 6)
@@ -494,7 +492,10 @@
     )(rows, send_a, got_a, got_b)
     got_c = swap(send_c, exchange_pairs(sizes, 1, False))
     got_d = swap(send_d, exchange_pairs(sizes, 1, True))
-    turns = tuple(range(sizes[1] - 1)) if sizes[1] in (2, 4) else ()
+    turns = ()
+    if sizes[1] in (2, 4):
+        reach = [max(abs(a - b) for a, b in round_pairs((1, sizes[1]), t)) for t in range(sizes[1] - 1)]
+        turns = tuple(sorted(range(sizes[1] - 1), key=lambda turn: -reach[turn]))
     size = capacity * 13
     out_shape = (shape(size, slots),) * (len(turns) + 1) if turns else (shape(sizes[1], size, slots),)
     flat = lambda kind, *dims: jax.ShapeDtypeStruct(dims, kind)

time: 21.9 us -> 20.7 us (0.945)
  waiting for transfers between devices: 7.68 us -> 6.55 us
    ppermute x7, waiting for transfers between devices: 7.68 us -> 6.55 us  [swap(): return lax.ppermute(value, ('gx', 'gy'), pairs)]
  transfers between devices with their start and end apart: 7 -> 7, of which waited for: 5 -> 4; matrix products, arithmetic and copies ran while one was open for 0% -> 0% of each run, Pallas kernels for 2% -> 2%
where the time goes in v4:
time: 20.7 us; the launch traced here: 20.5 us
  starting transfers between devices  10.5 us (51%)
  waiting for transfers between devices  6.55 us (32%)
  Pallas kernels  3.41 us (16%)
    ppermute x7, starting transfers between devices, swap(): return lax.ppermute(value, ('gx', 'gy'), pairs)  10.5 us
    ppermute x7, waiting for transfers between devices, swap(): return lax.ppermute(value, ('gx', 'gy'), pairs)  6.55 us
    pallas_call x1, Pallas kernels, per_device(): pl.pallas_call(functools.partial(force_kernel, counts=sizes, cells_x=cell...  1.24 us
    pallas_call x1, Pallas kernels, per_device(): pl.pallas_call(functools.partial(prepare_kernel, capacity=capacity), out_...  1.16 us
    pallas_call x1, Pallas kernels, per_device(): pl.pallas_call(functools.partial(gather_kernel, count=sizes[1], capacity=...  0.64 us
  transfers between devices with their start and end apart: 7, of which 4 were waited for; matrix products, arithmetic and copies ran while one was open for 0% of the time, Pallas kernels for 2%

profile of v4, /device:TPU:0, one launch (start us, length us, event | category | flops | bytes accessed | tf_op | source)
XLA Modules:
  0.0 20.5 jit_solution(6707443115855470866)
XLA Ops:
  0.0 1.2 %prepare.1 = (f32[32,128]{1,0:T(8,128)S(1)}, f32[32,128]{1,0:T(8,128)S(1)}, f32[32,128]{1,0:T(8,128)S(1)}) custom-call(f32[3,2,2,128]{3,2,1,0:T(2,128)} %refs_0_.1, f32[3,2,2,128]{3,2,1,0:T(2,128)} %refs_1_.1, f32[3,2,2,128]{3,2,1,0:T(2,128)} %refs_2_.1, s32[2,2,128]{2,1,0:T(2,128)} %refs_3_.1, s32[2,2]{1,0:T(2,128)} %refs_4_.1, s32[8,2,2,128]{3,2,1,0:T(2,128)} %lists.1, ...), custom_call_target="tpu_custom_call" | custom-call | tf_op jit(solution)/shard_map/prepare/pallas_call | solution.py:472
  1.2 3.1 %collective-permute-start.1 = (f32[32,128]{1,0:T(8,128)S(1)}, f32[32,128]{1,0:T(8,128)S(1)}, u32[]{:S(2)}, u32[]{:S(2)}) collective-permute-start(f32[32,128]{1,0:T(8,128)S(1)} %get-tuple-element.23), channel_id=1, source_target_pairs={{0,1},{1,0},{2,3},{3,2},{4,8},{5,9},{6,10},{7,11},{8,4},{9,5},{10,... | collective-permute-start | bytes 49160 | tf_op jit(solution)/shard_map/ppermute | solution.py:469
  4.3 0.0 collective-permute-start
  4.3 1.7 %collective-permute-done.1.got_b = f32[32,128]{1,0:T(8,128)S(1)} collective-permute-done((f32[32,128]{1,0:T(8,128)S(1)}, f32[32,128]{1,0:T(8,128)S(1)}, u32[]{:S(2)}, u32[]{:S(2)}) %collective-permute-start.1) | collective-permute-done | bytes 16416 | tf_op jit(solution)/shard_map/ppermute | solution.py:469
  6.0 0.0 collective-permute-done.got_a
  6.0 0.0 copy-start
  6.0 2.1 %collective-permute-start.2 = (f32[26,128]{1,0:T(8,128)S(1)}, f32[26,128]{1,0:T(8,128)S(1)}, u32[]{:S(2)}, u32[]{:S(2)}) collective-permute-start(f32[26,128]{1,0:T(8,128)S(1)} %get-tuple-element.31), channel_id=1, source_target_pairs={{0,1},{1,0},{2,3},{3,2},{4,5},{5,4},{6,7},{7,6},{8,9},{9,8},{10,11... | collective-permute-start | bytes 39944 | tf_op jit(solution)/shard_map/ppermute | solution.py:469
  8.1 0.0 collective-permute-start.3
  8.1 0.0 copy-done
  8.1 0.4 %near.1 = (f32[4,8,128]{2,1,0:T(8,128)S(1)}, f32[8,3,8,128]{3,2,1,0:T(8,128)S(1)}, s32[8,8,128]{2,1,0:T(8,128)S(1)}, s32[8,8,128]{2,1,0:T(8,128)S(1)}, f32[64,128]{1,0:T(8,128)S(1)}, /*index=5*/f32[64,128]{1,0:T(8,128)S(1)}) custom-call(f32[4,2,6,128]{3,2,1,0:T(8,128)S(1)} %get-tuple-element.24.middle, f32[32,128]{1,0:T(8,128)S(1)} %collective-permute-done.got_a, ...), custom_call_target="tpu_custom_call" | custom-call | flops 1000000 | bytes 200000 | tf_op jit(solution)/shard_map/near/pallas_call | solution.py:502
  8.5 1.4 %collective-permute-done.2.got_c = f32[26,128]{1,0:T(8,128)S(1)} collective-permute-done((f32[26,128]{1,0:T(8,128)S(1)}, f32[26,128]{1,0:T(8,128)S(1)}, u32[]{:S(2)}, u32[]{:S(2)}) %collective-permute-start.2) | collective-permute-done | bytes 13344 | tf_op jit(solution)/shard_map/ppermute | solution.py:469
  9.8 0.0 collective-permute-done.3.got_d
  9.9 1.2 %forces.1 = (f32[26,128]{1,0:T(8,128)S(1)}, f32[26,128]{1,0:T(8,128)S(1)}, f32[26,128]{1,0:T(8,128)S(1)}, f32[26,128]{1,0:T(8,128)S(1)}) custom-call(f32[32,128]{1,0:T(8,128)S(1)} %get-tuple-element.21.rows, f32[4,8,128]{2,1,0:T(8,128)S(1)} %get-tuple-element.25.centre, f32[8,3,8,128]{3,2,1,0:T(8,128)S(1)} %get-tuple-element.26.nearby_own, ...), custom_call_target="tpu_custom_call" | custom-call | tf_op jit(solution)/shard_map/forces/pallas_call | solution.py:522
  11.1 4.1 %collective-permute-start.4 = (f32[26,128]{1,0:T(8,128)S(1)}, f32[26,128]{1,0:T(8,128)S(1)}, u32[]{:S(2)}, u32[]{:S(2)}) collective-permute-start(f32[26,128]{1,0:T(8,128)S(1)} %get-tuple-element.33), channel_id=1, source_target_pairs={{0,3},{1,2},{2,1},{3,0},{4,7},{5,6},{6,5},{7,4},{8,11},{9,10},{10,... | collective-permute-start | bytes 39944 | tf_op jit(solution)/shard_map/ppermute | solution.py:469
  15.2 0.6 %collective-permute-start.5 = (f32[26,128]{1,0:T(8,128)S(1)}, f32[26,128]{1,0:T(8,128)S(1)}, u32[]{:S(2)}, u32[]{:S(2)}) collective-permute-start(f32[26,128]{1,0:T(8,128)S(1)} %get-tuple-element.34), channel_id=1, source_target_pairs={{0,2},{1,3},{2,0},{3,1},{4,6},{5,7},{6,4},{7,5},{8,10},{9,11},{10,... | collective-permute-start | bytes 39944 | tf_op jit(solution)/shard_map/ppermute | solution.py:469
  15.9 0.5 %collective-permute-start.6 = (f32[26,128]{1,0:T(8,128)S(1)}, f32[26,128]{1,0:T(8,128)S(1)}, u32[]{:S(2)}, u32[]{:S(2)}) collective-permute-start(f32[26,128]{1,0:T(8,128)S(1)} %get-tuple-element.35), channel_id=1, source_target_pairs={{0,1},{1,0},{2,3},{3,2},{4,5},{5,4},{6,7},{7,6},{8,9},{9,8},{10,11... | collective-permute-start | bytes 39944 | tf_op jit(solution)/shard_map/ppermute | solution.py:469
  16.3 0.7 %collective-permute-done.4.refs_0_ = f32[26,128]{1,0:T(8,128)S(1)} collective-permute-done((f32[26,128]{1,0:T(8,128)S(1)}, f32[26,128]{1,0:T(8,128)S(1)}, u32[]{:S(2)}, u32[]{:S(2)}) %collective-permute-start.4) | collective-permute-done | bytes 13344 | tf_op jit(solution)/shard_map/ppermute | solution.py:469
  17.0 2.8 %collective-permute-done.5.refs_1_ = f32[26,128]{1,0:T(8,128)S(1)} collective-permute-done((f32[26,128]{1,0:T(8,128)S(1)}, f32[26,128]{1,0:T(8,128)S(1)}, u32[]{:S(2)}, u32[]{:S(2)}) %collective-permute-start.5) | collective-permute-done | bytes 13344 | tf_op jit(solution)/shard_map/ppermute | solution.py:469
  19.8 0.0 collective-permute-done.6.refs_2_
  19.8 0.6 %collect.1 = f32[4,7,2,128]{3,2,1,0:T(2,128)} custom-call(f32[26,128]{1,0:T(8,128)S(1)} %collective-permute-done.4.refs_0_, f32[26,128]{1,0:T(8,128)S(1)} %collective-permute-done.5.refs_1_, f32[26,128]{1,0:T(8,128)S(1)} %collective-permute-done.6.refs_2_, f32[26,128]{1,0:T(8,128)S(1)} %get-tuple-element.36.refs_3_), custom_call_target="tpu_custom_call" | custom-call | tf_op jit(solution)/shard_map/collect/pallas_call | solution.py:545
  (1 shorter events, 0.0 us)
Async XLA Ops:
  1.2 4.8 %collective-permute-start.1 = (f32[32,128]{1,0:T(8,128)S(1)}, f32[32,128]{1,0:T(8,128)S(1)}, u32[]{:S(2)}, u32[]{:S(2)}) collective-permute-start(f32[32,128]{1,0:T(8,128)S(1)} %get-tuple-element.23), channel_id=1, source_target_pairs={{0,1},{1,0},{2,3},{3,2},{4,8},{5,9},{6,10},{7,11},{8,4},{9,5},{10,... | collective-permute-start | bytes 49160 | tf_op jit(solution)/shard_map/ppermute | solution.py:469
  4.3 1.7 %collective-permute-start = (f32[32,128]{1,0:T(8,128)S(1)}, f32[32,128]{1,0:T(8,128)S(1)}, u32[]{:S(2)}, u32[]{:S(2)}) collective-permute-start(f32[32,128]{1,0:T(8,128)S(1)} %get-tuple-element.22.own), channel_id=1, source_target_pairs={{0,4},{1,5},{2,6},{3,7},{4,0},{5,1},{6,2},{7,3},{8,12},{9,13},{10,... | collective-permute-start | bytes 49160 | tf_op jit(solution)/shard_map/ppermute | solution.py:469
  6.0 2.1 %copy-start = (s32[8,2,2,128]{3,2,1,0:T(2,128)S(1)}, s32[8,2,2,128]{3,2,1,0:T(2,128)}, u32[]{:S(2)}) copy-start(s32[8,2,2,128]{3,2,1,0:T(2,128)} %lists.1) | copy-start | bytes 49156
  6.0 3.8 %collective-permute-start.2 = (f32[26,128]{1,0:T(8,128)S(1)}, f32[26,128]{1,0:T(8,128)S(1)}, u32[]{:S(2)}, u32[]{:S(2)}) collective-permute-start(f32[26,128]{1,0:T(8,128)S(1)} %get-tuple-element.31), channel_id=1, source_target_pairs={{0,1},{1,0},{2,3},{3,2},{4,5},{5,4},{6,7},{7,6},{8,9},{9,8},{10,11... | collective-permute-start | bytes 39944 | tf_op jit(solution)/shard_map/ppermute | solution.py:469
  8.1 1.7 %collective-permute-start.3 = (f32[26,128]{1,0:T(8,128)S(1)}, f32[26,128]{1,0:T(8,128)S(1)}, u32[]{:S(2)}, u32[]{:S(2)}) collective-permute-start(f32[26,128]{1,0:T(8,128)S(1)} %get-tuple-element.32), channel_id=1, source_target_pairs={{0,4},{1,2},{2,1},{3,7},{4,0},{5,6},{6,5},{7,3},{8,12},{9,10},{10,... | collective-permute-start | bytes 39944 | tf_op jit(solution)/shard_map/ppermute | solution.py:469
  11.1 5.9 %collective-permute-start.4 = (f32[26,128]{1,0:T(8,128)S(1)}, f32[26,128]{1,0:T(8,128)S(1)}, u32[]{:S(2)}, u32[]{:S(2)}) collective-permute-start(f32[26,128]{1,0:T(8,128)S(1)} %get-tuple-element.33), channel_id=1, source_target_pairs={{0,3},{1,2},{2,1},{3,0},{4,7},{5,6},{6,5},{7,4},{8,11},{9,10},{10,... | collective-permute-start | bytes 39944 | tf_op jit(solution)/shard_map/ppermute | solution.py:469
  15.2 4.6 %collective-permute-start.5 = (f32[26,128]{1,0:T(8,128)S(1)}, f32[26,128]{1,0:T(8,128)S(1)}, u32[]{:S(2)}, u32[]{:S(2)}) collective-permute-start(f32[26,128]{1,0:T(8,128)S(1)} %get-tuple-element.34), channel_id=1, source_target_pairs={{0,2},{1,3},{2,0},{3,1},{4,6},{5,7},{6,4},{7,5},{8,10},{9,11},{10,... | collective-permute-start | bytes 39944 | tf_op jit(solution)/shard_map/ppermute | solution.py:469
  15.9 4.0 %collective-permute-start.6 = (f32[26,128]{1,0:T(8,128)S(1)}, f32[26,128]{1,0:T(8,128)S(1)}, u32[]{:S(2)}, u32[]{:S(2)}) collective-permute-start(f32[26,128]{1,0:T(8,128)S(1)} %get-tuple-element.35), channel_id=1, source_target_pairs={{0,1},{1,0},{2,3},{3,2},{4,5},{5,4},{6,7},{7,6},{8,9},{9,8},{10,11... | collective-permute-start | bytes 39944 | tf_op jit(solution)/shard_map/ppermute | solution.py:469

commit v5 on v4

--- a/solution.py
+++ b/solution.py
@@ -69,30 +69,33 @@
     return pairs
 
 
-def prepare_kernel(*refs, capacity):
-    count = 7
-    sources, (rows, send_a, send_b) = refs[:count], refs[count : count + 3]
-    held, done = refs[count + 3 : -1], refs[-1]
-    copies = [
-        pltpu.make_async_copy(source, target, done.at[n])
-        for n, (source, target) in enumerate(zip(sources, held))
-    ]
-    for copy in copies:
-        copy.start()
-    disp, vel, force, heights, counts, lists, plan = held
-    _, cells_x, cells_y, slots = disp.shape
-    entries = lists.shape[0]
+def prepare_kernel(
+    disp_in, vel_in, force_in, heights_in, counts_in, lists_in, plan_in,
+    rows, send_a, send_b, motion, layers, counts, plan, done, *, capacity
+):
+    _, cells_x, cells_y, slots = disp_in.shape
+    entries = lists_in.shape[0]
+    for n, source in enumerate((disp_in, vel_in, force_in)):
+        pltpu.make_async_copy(source, motion.at[n], done.at[0]).start()
+    pltpu.make_async_copy(counts_in, counts, done.at[2]).start()
+    pltpu.make_async_copy(plan_in, plan, done.at[3]).start()
+    pltpu.make_async_copy(heights_in, layers.at[entries], done.at[1]).start()
+    pltpu.make_async_copy(lists_in, layers.at[pl.ds(0, entries)], done.at[1]).start()
     at_x, at_y = lax.axis_index("gx"), lax.axis_index("gy")
     even_x = lax.rem(at_x, 2) == 0
-    for copy in copies:
-        copy.wait()
-    owners = [plan[:, c : c + 1] for c in range(cells_x * cells_y)]
+    pltpu.make_async_copy(motion, motion, done.at[0]).wait()
+    pltpu.make_async_copy(layers, layers, done.at[1]).wait()
+    pltpu.make_async_copy(counts_in, counts, done.at[2]).wait()
+    pltpu.make_async_copy(plan_in, plan, done.at[3]).wait()
+    disp, vel, force = motion.at[0], motion.at[1], motion.at[2]
+    heights, lists = layers.at[entries], layers
+    owners = [plan[0, c] for c in range(cells_x * cells_y)]
     for x in range(cells_x):
         base_x = ((at_x * cells_x + x).astype(jnp.float32) + 0.5) * spacing
         for y in range(cells_y):
             base_y = ((at_y * cells_y + y).astype(jnp.float32) + 0.5) * spacing
             layer = heights[x, pl.ds(y, 1), :]
-            occupied = (layer < counts[x : x + 1, y : y + 1]).astype(jnp.float32)
+            occupied = (layer < counts[x, y]).astype(jnp.float32)
             lattice = (base_x, base_y, (layer.astype(jnp.float32) + 0.5) * spacing)
             column = (x * cells_y + y) * ROWS
             for q in range(3):
@@ -108,8 +111,8 @@
             rows[pl.ds(column + 6, 1), :] = occupied
             owner = owners[x * cells_y + y]
             earlier = sum((owners[c] == owner).astype(jnp.int32) for c in range(x * cells_y + y))
-            rows[pl.ds(column + 7, 1), :] = jnp.broadcast_to(
-                (owner * capacity + earlier).astype(jnp.float32), (1, slots)
+            rows[pl.ds(column + 7, 1), :] = jnp.full(
+                (1, slots), jnp.asarray(owner * capacity + earlier, jnp.int32).astype(jnp.float32)
             )
             place = (3 * cells_y + y) * cells_x + x
             send_a[pl.ds(place, 1), :] = occupied
@@ -122,7 +125,7 @@
         send_b[pl.ds(base + m * cells_y, cells_y), :] = jnp.where(even_x, low, high)
 
 
-def strip_kernel(rows, own, got_a, got_b, middle, send_c, send_d, *, count_x, cells_x, cells_y):
+def strip_kernel(own, got_a, got_b, middle, send_c, send_d, *, count_x, cells_x, cells_y):
     at_x, at_y = lax.axis_index("gx"), lax.axis_index("gy")
     even_x, even_y = lax.rem(at_x, 2) == 0, lax.rem(at_y, 2) == 0
     has_left = (at_x > 0).astype(jnp.float32)
@@ -141,11 +144,6 @@
         low, high = middle[q, 0], middle[q, cells_y - 1]
         send_c[pl.ds(q * wide, wide), :] = jnp.where(even_y, high, low)
         send_d[pl.ds(q * wide, wide), :] = jnp.where(even_y, low, high)
-    for x in range(cells_x):
-        low = rows[pl.ds(x * cells_y * ROWS + 7, 1), :]
-        high = rows[pl.ds((x * cells_y + cells_y - 1) * ROWS + 7, 1), :]
-        send_c[pl.ds(4 * wide + x, 1), :] = jnp.where(even_y, high, low)
-        send_d[pl.ds(4 * wide + x, 1), :] = jnp.where(even_y, low, high)
 
 
 def half_wave(radius):
@@ -288,7 +286,7 @@
     counts, cells_x, cells_y, capacity, turns
 ):
     outs = refs[: len(turns) + 1] if turns else refs[:1]
-    table, parts, main, ghost = refs[len(outs) :]
+    table, parts = refs[len(outs) :]
     entries, centers, slots = slot_at.shape
     at_y = lax.axis_index("gy")
     even_y = lax.rem(at_y, 2) == 0
@@ -379,6 +377,7 @@
     line = lax.broadcasted_iota(jnp.int32, (ROWS, slots), 0)
     kick = half_step * force_scale
     chosen = (line >= 3) & (line < 6)
+    columns, ghosts = [], []
     for x in range(cells_x):
         for y in range(-1, cells_y + 1):
             block = reached[x, y]
@@ -387,33 +386,17 @@
                 block = column_parts(entries, y * near + x + 1) - block
                 column = rows[pl.ds((x * cells_y + y) * ROWS, ROWS), :]
                 column = column + jnp.where(chosen, kick * block, 0.0)
-                main[x * cells_y + y] = column
+                named = jnp.broadcast_to(column[7:], (ROWS, slots))
+                columns.append((named, jnp.where(line == 7, float(x * cells_y + y + 1), column)))
             else:
-                ghost[0 if y < 0 else 1, x] = -kick * block
-    places = [4 * wide + x for x in range(cells_x)]
-    below = [jnp.where(even_y, got_d[pl.ds(p, 1), :], got_c[pl.ds(p, 1), :]) for p in places]
-    above = [jnp.where(even_y, got_c[pl.ds(p, 1), :], got_d[pl.ds(p, 1), :]) for p in places]
-    columns = [main[c] for c in range(cells_x * cells_y)]
-    named_here = [
-        jnp.broadcast_to(main[c, pl.ds(7, 1), :], (ROWS, slots)) for c in range(cells_x * cells_y)
-    ]
+                ghosts.append((-kick * block)[3:6])
 
     def message(owner):
         pieces = []
         for slot in range(capacity):
             wanted = (owner * capacity + slot).astype(jnp.float32)
-            piece = 0.0
-            for column, named in zip(columns, named_here):
-                piece = piece + jnp.where(named == wanted, column, 0.0)
-            pieces.append(piece[:7])
-        for side, named in enumerate((below, above)):
-            for slot in range(capacity):
-                wanted = (owner * capacity + slot).astype(jnp.float32)
-                piece = 0.0
-                for x in range(cells_x):
-                    piece = piece + jnp.where(named[x] == wanted, ghost[side, x, pl.ds(3, 3), :], 0.0)
-                pieces.append(piece)
-        return pieces
+            pieces.append(sum(jnp.where(named == wanted, column, 0.0) for named, column in columns))
+        return pieces + ghosts
 
     def write(ref, pieces):
         first = 0
@@ -430,7 +413,7 @@
             write(outs[0].at[owner], message(jnp.int32(owner)))
 
 
-def gather_kernel(*refs, count, capacity, turns):
+def gather_kernel(*refs, count, cells_x, cells_y, capacity, turns):
     at_y = lax.axis_index("gy")
     if turns:
         ins, out, held = refs[:-2], refs[-2], refs[-1]
@@ -439,15 +422,17 @@
         held[at_y] = ins[-1][...]
     else:
         held, out = refs
-    first = capacity * 7
+    first = capacity * ROWS
     for source in range(count):
         for slot in range(capacity):
-            block = held[source, pl.ds(slot * 7, 7), :]
+            block = held[source, pl.ds(slot * ROWS, ROWS), :]
+            name = held[source, pl.ds(slot * ROWS + 7, 3, stride=0), :]
             speed = block[3:6]
-            if source + 1 < count:
-                speed = speed + held[source + 1, pl.ds(first + slot * 3, 3), :]
-            if source > 0:
-                speed = speed + held[source - 1, pl.ds(first + (capacity + slot) * 3, 3), :]
+            for x in range(cells_x):
+                for other, y, side in ((source + 1, cells_y - 1, 0), (source - 1, 0, 1)):
+                    if 0 <= other < count:
+                        part = held[other, pl.ds(first + (2 * x + side) * 3, 3), :]
+                        speed = speed + jnp.where(name == float(x * cells_y + y + 1), part, 0.0)
             for line in range(7):
                 value = speed[line - 3 : line - 2] if 3 <= line < 6 else block[line : line + 1]
                 out[source, line, pl.ds(slot, 1), :] = value
@@ -474,29 +459,34 @@
         out_shape=(shape(columns * ROWS, slots), shape(first_size, slots), shape(first_size, slots)),
         in_specs=[pl.BlockSpec(memory_space=HBM)] * len(inputs),
         out_specs=(whole, whole, whole),
-        scratch_shapes=[pltpu.VMEM(value.shape, value.dtype) for value in inputs]
-        + [pltpu.SemaphoreType.DMA((len(inputs),))],
+        scratch_shapes=[
+            pltpu.VMEM((3,) + displacement.shape, jnp.float32),
+            pltpu.VMEM((entries + 1,) + heights.shape, jnp.int32),
+            pltpu.SMEM(counts.shape, jnp.int32),
+            pltpu.SMEM((1, columns), jnp.int32),
+            pltpu.SemaphoreType.DMA((4,)),
+        ],
         compiler_params=pltpu.CompilerParams(vmem_limit_bytes=VMEM_BYTES),
         name="prepare",
     )(*[pltpu.with_memory_space_constraint(value, HBM) for value in inputs])
     got_a = swap(send_a, exchange_pairs(sizes, 0, False))
     got_b = swap(send_b, exchange_pairs(sizes, 0, True))
-    second_size = 4 * wide + cells_x
+    second_size = 4 * wide
     middle, send_c, send_d = pl.pallas_call(
         functools.partial(strip_kernel, count_x=sizes[0], cells_x=cells_x, cells_y=cells_y),
         out_shape=(shape(4, cells_y, wide, slots), shape(second_size, slots), shape(second_size, slots)),
-        in_specs=[whole] * 4,
+        in_specs=[whole] * 3,
         out_specs=(whole, whole, whole),
         compiler_params=pltpu.CompilerParams(vmem_limit_bytes=VMEM_BYTES),
         name="strips",
-    )(rows, send_a, got_a, got_b)
+    )(send_a, got_a, got_b)
     got_c = swap(send_c, exchange_pairs(sizes, 1, False))
     got_d = swap(send_d, exchange_pairs(sizes, 1, True))
     turns = ()
     if sizes[1] in (2, 4):
         reach = [max(abs(a - b) for a, b in round_pairs((1, sizes[1]), t)) for t in range(sizes[1] - 1)]
         turns = tuple(sorted(range(sizes[1] - 1), key=lambda turn: -reach[turn]))
-    size = capacity * 13
+    size = capacity * ROWS + 6 * cells_x
     out_shape = (shape(size, slots),) * (len(turns) + 1) if turns else (shape(sizes[1], size, slots),)
     flat = lambda kind, *dims: jax.ShapeDtypeStruct(dims, kind)
     found = pl.pallas_call(
@@ -529,8 +519,6 @@
         scratch_shapes=[
             pltpu.VMEM((3, 3, centers, slots), jnp.float32),
             pltpu.VMEM(((entries + 1) * ROWS * centers, slots), jnp.float32),
-            pltpu.VMEM((columns, ROWS, slots), jnp.float32),
-            pltpu.VMEM((2, cells_x, ROWS, slots), jnp.float32),
         ],
         compiler_params=pltpu.CompilerParams(vmem_limit_bytes=VMEM_BYTES),
         name="forces",
@@ -543,7 +531,9 @@
         arrived = [lax.all_to_all(sent[0], "gy", split_axis=0, concat_axis=0, tiled=True)]
         scratch = []
     result = pl.pallas_call(
-        functools.partial(gather_kernel, count=sizes[1], capacity=capacity, turns=turns),
+        functools.partial(
+            gather_kernel, count=sizes[1], cells_x=cells_x, cells_y=cells_y, capacity=capacity, turns=turns
+        ),
         out_shape=shape(sizes[1], 7, capacity, slots),
         in_specs=[whole] * len(arrived),
         out_specs=whole,

time: 20.7 us -> 20.4 us (0.986)
  Pallas kernels: 3.41 us -> 3.14 us
    pallas_call x1, Pallas kernels: 1.16 us -> 0.9 us  [per_device(): pl.pallas_call(functools.partial(prepare_kernel, capacity=capacity), out_...]
where the time goes in v5:
time: 20.4 us; the launch traced here: 20.2 us
  starting transfers between devices  10.5 us (51%)
  waiting for transfers between devices  6.52 us (32%)
  Pallas kernels  3.14 us (15%)
    ppermute x7, starting transfers between devices, swap(): return lax.ppermute(value, ('gx', 'gy'), pairs)  10.5 us
    ppermute x7, waiting for transfers between devices, swap(): return lax.ppermute(value, ('gx', 'gy'), pairs)  6.52 us
    pallas_call x1, Pallas kernels, per_device(): pl.pallas_call(functools.partial(force_kernel, counts=sizes, cells_x=cell...  1.22 us
    pallas_call x1, Pallas kernels, per_device(): pl.pallas_call(functools.partial(prepare_kernel, capacity=capacity), out_...  0.9 us
    pallas_call x1, Pallas kernels, per_device(): pl.pallas_call(functools.partial(gather_kernel, count=sizes[1], cells_x=c...  0.64 us
  transfers between devices with their start and end apart: 7, of which 4 were waited for; matrix products, arithmetic and copies ran while one was open for 0% of the time, Pallas kernels for 2%

profile of v5, /device:TPU:0, one launch (start us, length us, event | category | flops | bytes accessed | tf_op | source)
XLA Modules:
  0.0 20.2 jit_solution(2204433584495623882)
XLA Ops:
  0.0 0.9 %prepare.1 = (f32[32,128]{1,0:T(8,128)S(1)}, f32[32,128]{1,0:T(8,128)S(1)}, f32[32,128]{1,0:T(8,128)S(1)}) custom-call(f32[3,2,2,128]{3,2,1,0:T(2,128)} %disp_in.1, f32[3,2,2,128]{3,2,1,0:T(2,128)} %vel_in.1, f32[3,2,2,128]{3,2,1,0:T(2,128)} %force_in.1, s32[2,2,128]{2,1,0:T(2,128)} %heights_in.1, s32[2,2]{1,0:T(2,128)} %counts_in.1, ...), custom_call_target="tpu_custom_call" | custom-call | tf_op jit(solution)/shard_map/prepare/pallas_call | solution.py:457
  0.9 3.1 %collective-permute-start.1 = (f32[32,128]{1,0:T(8,128)S(1)}, f32[32,128]{1,0:T(8,128)S(1)}, u32[]{:S(2)}, u32[]{:S(2)}) collective-permute-start(f32[32,128]{1,0:T(8,128)S(1)} %get-tuple-element.23), channel_id=1, source_target_pairs={{0,1},{1,0},{2,3},{3,2},{4,8},{5,9},{6,10},{7,11},{8,4},{9,5},{10,... | collective-permute-start | bytes 49160 | tf_op jit(solution)/shard_map/ppermute | solution.py:454
  4.0 0.0 copy-start
  4.0 0.0 collective-permute-start
  4.1 1.7 %collective-permute-done.1.got_b = f32[32,128]{1,0:T(8,128)S(1)} collective-permute-done((f32[32,128]{1,0:T(8,128)S(1)}, f32[32,128]{1,0:T(8,128)S(1)}, u32[]{:S(2)}, u32[]{:S(2)}) %collective-permute-start.1) | collective-permute-done | bytes 16416 | tf_op jit(solution)/shard_map/ppermute | solution.py:454
  5.7 0.0 collective-permute-done.got_a
  5.8 2.1 %collective-permute-start.2 = (f32[24,128]{1,0:T(8,128)S(1)}, f32[24,128]{1,0:T(8,128)S(1)}, u32[]{:S(2)}, u32[]{:S(2)}) collective-permute-start(f32[24,128]{1,0:T(8,128)S(1)} %get-tuple-element.31), channel_id=1, source_target_pairs={{0,1},{1,0},{2,3},{3,2},{4,5},{5,4},{6,7},{7,6},{8,9},{9,8},{10,11... | collective-permute-start | bytes 36872 | tf_op jit(solution)/shard_map/ppermute | solution.py:454
  7.9 0.0 collective-permute-start.3
  7.9 0.0 copy-done
  7.9 0.4 %near.1 = (f32[4,8,128]{2,1,0:T(8,128)S(1)}, f32[8,3,8,128]{3,2,1,0:T(8,128)S(1)}, s32[8,8,128]{2,1,0:T(8,128)S(1)}, s32[8,8,128]{2,1,0:T(8,128)S(1)}, f32[64,128]{1,0:T(8,128)S(1)}, /*index=5*/f32[64,128]{1,0:T(8,128)S(1)}) custom-call(f32[4,2,6,128]{3,2,1,0:T(8,128)S(1)} %get-tuple-element.24.middle, f32[32,128]{1,0:T(8,128)S(1)} %collective-permute-done.got_a, ...), custom_call_target="tpu_custom_call" | custom-call | flops 1000000 | bytes 200000 | tf_op jit(solution)/shard_map/near/pallas_call | solution.py:492
  8.2 1.3 %collective-permute-done.2.got_c = f32[24,128]{1,0:T(8,128)S(1)} collective-permute-done((f32[24,128]{1,0:T(8,128)S(1)}, f32[24,128]{1,0:T(8,128)S(1)}, u32[]{:S(2)}, u32[]{:S(2)}) %collective-permute-start.2) | collective-permute-done | bytes 12320 | tf_op jit(solution)/shard_map/ppermute | solution.py:454
  9.5 0.0 collective-permute-done.3.got_d
  9.5 1.2 %forces.1 = (f32[28,128]{1,0:T(8,128)S(1)}, f32[28,128]{1,0:T(8,128)S(1)}, f32[28,128]{1,0:T(8,128)S(1)}, f32[28,128]{1,0:T(8,128)S(1)}) custom-call(f32[32,128]{1,0:T(8,128)S(1)} %get-tuple-element.21.rows, f32[4,8,128]{2,1,0:T(8,128)S(1)} %get-tuple-element.25.centre, f32[8,3,8,128]{3,2,1,0:T(8,128)S(1)} %get-tuple-element.26.nearby_own, ...), custom_call_target="tpu_custom_call" | custom-call | tf_op jit(solution)/shard_map/forces/pallas_call | solution.py:512
  10.8 4.1 %collective-permute-start.4 = (f32[28,128]{1,0:T(8,128)S(1)}, f32[28,128]{1,0:T(8,128)S(1)}, u32[]{:S(2)}, u32[]{:S(2)}) collective-permute-start(f32[28,128]{1,0:T(8,128)S(1)} %get-tuple-element.33), channel_id=1, source_target_pairs={{0,3},{1,2},{2,1},{3,0},{4,7},{5,6},{6,5},{7,4},{8,11},{9,10},{10,... | collective-permute-start | bytes 43016 | tf_op jit(solution)/shard_map/ppermute | solution.py:454
  14.9 0.6 %collective-permute-start.5 = (f32[28,128]{1,0:T(8,128)S(1)}, f32[28,128]{1,0:T(8,128)S(1)}, u32[]{:S(2)}, u32[]{:S(2)}) collective-permute-start(f32[28,128]{1,0:T(8,128)S(1)} %get-tuple-element.34), channel_id=1, source_target_pairs={{0,2},{1,3},{2,0},{3,1},{4,6},{5,7},{6,4},{7,5},{8,10},{9,11},{10,... | collective-permute-start | bytes 43016 | tf_op jit(solution)/shard_map/ppermute | solution.py:454
  15.5 0.5 %collective-permute-start.6 = (f32[28,128]{1,0:T(8,128)S(1)}, f32[28,128]{1,0:T(8,128)S(1)}, u32[]{:S(2)}, u32[]{:S(2)}) collective-permute-start(f32[28,128]{1,0:T(8,128)S(1)} %get-tuple-element.35), channel_id=1, source_target_pairs={{0,1},{1,0},{2,3},{3,2},{4,5},{5,4},{6,7},{7,6},{8,9},{9,8},{10,11... | collective-permute-start | bytes 43016 | tf_op jit(solution)/shard_map/ppermute | solution.py:454
  16.0 0.7 %collective-permute-done.4.refs_0_ = f32[28,128]{1,0:T(8,128)S(1)} collective-permute-done((f32[28,128]{1,0:T(8,128)S(1)}, f32[28,128]{1,0:T(8,128)S(1)}, u32[]{:S(2)}, u32[]{:S(2)}) %collective-permute-start.4) | collective-permute-done | bytes 14368 | tf_op jit(solution)/shard_map/ppermute | solution.py:454
  16.7 2.8 %collective-permute-done.5.refs_1_ = f32[28,128]{1,0:T(8,128)S(1)} collective-permute-done((f32[28,128]{1,0:T(8,128)S(1)}, f32[28,128]{1,0:T(8,128)S(1)}, u32[]{:S(2)}, u32[]{:S(2)}) %collective-permute-start.5) | collective-permute-done | bytes 14368 | tf_op jit(solution)/shard_map/ppermute | solution.py:454
  19.5 0.0 collective-permute-done.6.refs_2_
  19.5 0.6 %collect.1 = f32[4,7,2,128]{3,2,1,0:T(2,128)} custom-call(f32[28,128]{1,0:T(8,128)S(1)} %collective-permute-done.4.refs_0_, f32[28,128]{1,0:T(8,128)S(1)} %collective-permute-done.5.refs_1_, f32[28,128]{1,0:T(8,128)S(1)} %collective-permute-done.6.refs_2_, f32[28,128]{1,0:T(8,128)S(1)} %get-tuple-element.36.refs_3_), custom_call_target="tpu_custom_call" | custom-call | tf_op jit(solution)/shard_map/collect/pallas_call | solution.py:533
  (1 shorter events, 0.0 us)
Async XLA Ops:
  0.9 4.8 %collective-permute-start.1 = (f32[32,128]{1,0:T(8,128)S(1)}, f32[32,128]{1,0:T(8,128)S(1)}, u32[]{:S(2)}, u32[]{:S(2)}) collective-permute-start(f32[32,128]{1,0:T(8,128)S(1)} %get-tuple-element.23), channel_id=1, source_target_pairs={{0,1},{1,0},{2,3},{3,2},{4,8},{5,9},{6,10},{7,11},{8,4},{9,5},{10,... | collective-permute-start | bytes 49160 | tf_op jit(solution)/shard_map/ppermute | solution.py:454
  4.0 3.8 %copy-start = (s32[8,2,2,128]{3,2,1,0:T(2,128)S(1)}, s32[8,2,2,128]{3,2,1,0:T(2,128)}, u32[]{:S(2)}) copy-start(s32[8,2,2,128]{3,2,1,0:T(2,128)} %lists.1) | copy-start | bytes 49156
  4.0 1.7 %collective-permute-start = (f32[32,128]{1,0:T(8,128)S(1)}, f32[32,128]{1,0:T(8,128)S(1)}, u32[]{:S(2)}, u32[]{:S(2)}) collective-permute-start(f32[32,128]{1,0:T(8,128)S(1)} %get-tuple-element.22.own), channel_id=1, source_target_pairs={{0,4},{1,5},{2,6},{3,7},{4,0},{5,1},{6,2},{7,3},{8,12},{9,13},{10,... | collective-permute-start | bytes 49160 | tf_op jit(solution)/shard_map/ppermute | solution.py:454
  5.8 3.8 %collective-permute-start.2 = (f32[24,128]{1,0:T(8,128)S(1)}, f32[24,128]{1,0:T(8,128)S(1)}, u32[]{:S(2)}, u32[]{:S(2)}) collective-permute-start(f32[24,128]{1,0:T(8,128)S(1)} %get-tuple-element.31), channel_id=1, source_target_pairs={{0,1},{1,0},{2,3},{3,2},{4,5},{5,4},{6,7},{7,6},{8,9},{9,8},{10,11... | collective-permute-start | bytes 36872 | tf_op jit(solution)/shard_map/ppermute | solution.py:454
  7.9 1.7 %collective-permute-start.3 = (f32[24,128]{1,0:T(8,128)S(1)}, f32[24,128]{1,0:T(8,128)S(1)}, u32[]{:S(2)}, u32[]{:S(2)}) collective-permute-start(f32[24,128]{1,0:T(8,128)S(1)} %get-tuple-element.32), channel_id=1, source_target_pairs={{0,4},{1,2},{2,1},{3,7},{4,0},{5,6},{6,5},{7,3},{8,12},{9,10},{10,... | collective-permute-start | bytes 36872 | tf_op jit(solution)/shard_map/ppermute | solution.py:454
  10.8 5.9 %collective-permute-start.4 = (f32[28,128]{1,0:T(8,128)S(1)}, f32[28,128]{1,0:T(8,128)S(1)}, u32[]{:S(2)}, u32[]{:S(2)}) collective-permute-start(f32[28,128]{1,0:T(8,128)S(1)} %get-tuple-element.33), channel_id=1, source_target_pairs={{0,3},{1,2},{2,1},{3,0},{4,7},{5,6},{6,5},{7,4},{8,11},{9,10},{10,... | collective-permute-start | bytes 43016 | tf_op jit(solution)/shard_map/ppermute | solution.py:454
  14.9 4.6 %collective-permute-start.5 = (f32[28,128]{1,0:T(8,128)S(1)}, f32[28,128]{1,0:T(8,128)S(1)}, u32[]{:S(2)}, u32[]{:S(2)}) collective-permute-start(f32[28,128]{1,0:T(8,128)S(1)} %get-tuple-element.34), channel_id=1, source_target_pairs={{0,2},{1,3},{2,0},{3,1},{4,6},{5,7},{6,4},{7,5},{8,10},{9,11},{10,... | collective-permute-start | bytes 43016 | tf_op jit(solution)/shard_map/ppermute | solution.py:454
  15.5 4.0 %collective-permute-start.6 = (f32[28,128]{1,0:T(8,128)S(1)}, f32[28,128]{1,0:T(8,128)S(1)}, u32[]{:S(2)}, u32[]{:S(2)}) collective-permute-start(f32[28,128]{1,0:T(8,128)S(1)} %get-tuple-element.35), channel_id=1, source_target_pairs={{0,1},{1,0},{2,3},{3,2},{4,5},{5,4},{6,7},{7,6},{8,9},{9,8},{10,11... | collective-permute-start | bytes 43016 | tf_op jit(solution)/shard_map/ppermute | solution.py:454

commit v6 on v5

--- a/solution.py
+++ b/solution.py
@@ -51,22 +51,31 @@
     return pairs
 
 
-def round_partner(place, turn, count):
-    ring = count - 1
-    other = lax.rem(turn - place + 2 * ring, ring)
-    alone = turn * ((ring + 1) // 2) % ring
-    return jnp.where(place == ring, alone, jnp.where(place == alone, ring, other))
-
-
-def round_pairs(counts, turn):
-    ring = counts[1] - 1
-    alone = turn * ((ring + 1) // 2) % ring
+def circle_pairs(counts, rising):
     pairs = []
     for a in range(counts[0]):
         for b in range(counts[1]):
-            other = alone if b == ring else ring if b == alone else (turn - b) % ring
-            pairs.append((a * counts[1] + b, a * counts[1] + other))
+            other = (a, b + (1 if a % 2 == rising else -1))
+            if not 0 <= other[1] < counts[1]:
+                other = (a ^ 1, b)
+            if other[0] < counts[0]:
+                pairs.append((a * counts[1] + b, other[0] * counts[1] + other[1]))
     return pairs
+
+
+def rounds(count):
+    if count == 4:
+        circuit = (0, 2, 1, 3)
+        ahead, back = [
+            tuple(circuit[(circuit.index(place) + way) % count] for place in range(count))
+            for way in (1, -1)
+        ]
+        return (ahead, back, tuple(place ^ 1 for place in range(count)))
+    return ((1, 0),) if count == 2 else ()
+
+
+def named_by(table, place):
+    return sum(jnp.where(place == n, other, 0) for n, other in enumerate(table))
 
 
 def prepare_kernel(
@@ -126,8 +135,8 @@
 
 
 def strip_kernel(own, got_a, got_b, middle, send_c, send_d, *, count_x, cells_x, cells_y):
-    at_x, at_y = lax.axis_index("gx"), lax.axis_index("gy")
-    even_x, even_y = lax.rem(at_x, 2) == 0, lax.rem(at_y, 2) == 0
+    at_x = lax.axis_index("gx")
+    even_x = lax.rem(at_x, 2) == 0
     has_left = (at_x > 0).astype(jnp.float32)
     has_right = (at_x < count_x - 1).astype(jnp.float32)
     wide = cells_x + 4
@@ -142,8 +151,8 @@
             strip = jnp.concatenate([left, take(own), right], axis=0)
             middle[q, y] = strip
         low, high = middle[q, 0], middle[q, cells_y - 1]
-        send_c[pl.ds(q * wide, wide), :] = jnp.where(even_y, high, low)
-        send_d[pl.ds(q * wide, wide), :] = jnp.where(even_y, low, high)
+        send_c[pl.ds(q * wide, wide), :] = jnp.where(even_x, low, high)
+        send_d[pl.ds(q * wide, wide), :] = jnp.where(even_x, high, low)
 
 
 def half_wave(radius):
@@ -289,12 +298,12 @@
     table, parts = refs[len(outs) :]
     entries, centers, slots = slot_at.shape
     at_y = lax.axis_index("gy")
-    even_y = lax.rem(at_y, 2) == 0
+    even_x = lax.rem(lax.axis_index("gx"), 2) == 0
     wide, near = cells_x + 4, cells_x + 2
     has_below, has_above = at_y > 0, at_y < counts[1] - 1
     for row, swap, there in (
-        (0, even_y, has_below),
-        (centers - near, jnp.logical_not(even_y), has_above),
+        (0, even_x, has_below),
+        (centers - near, jnp.logical_not(even_x), has_above),
     ):
         strip = [
             jnp.where(swap, got_d[pl.ds(q * wide, wide), :], got_c[pl.ds(q * wide, wide), :])
@@ -406,7 +415,7 @@
 
     if turns:
         for ref, turn in zip(outs[:-1], turns):
-            write(ref, message(round_partner(at_y, turn, counts[1])))
+            write(ref, message(named_by(turn, at_y)))
         write(outs[-1], message(at_y))
     else:
         for owner in range(counts[1]):
@@ -418,7 +427,7 @@
     if turns:
         ins, out, held = refs[:-2], refs[-2], refs[-1]
         for ref, turn in zip(ins[:-1], turns):
-            held[round_partner(at_y, turn, count)] = ref[...]
+            held[named_by([turn.index(n) for n in range(count)], at_y)] = ref[...]
         held[at_y] = ins[-1][...]
     else:
         held, out = refs
@@ -480,12 +489,9 @@
         compiler_params=pltpu.CompilerParams(vmem_limit_bytes=VMEM_BYTES),
         name="strips",
     )(send_a, got_a, got_b)
-    got_c = swap(send_c, exchange_pairs(sizes, 1, False))
-    got_d = swap(send_d, exchange_pairs(sizes, 1, True))
-    turns = ()
-    if sizes[1] in (2, 4):
-        reach = [max(abs(a - b) for a, b in round_pairs((1, sizes[1]), t)) for t in range(sizes[1] - 1)]
-        turns = tuple(sorted(range(sizes[1] - 1), key=lambda turn: -reach[turn]))
+    got_c = swap(send_c, circle_pairs(sizes, 1))
+    got_d = swap(send_d, circle_pairs(sizes, 0))
+    turns = rounds(sizes[1])
     size = capacity * ROWS + 6 * cells_x
     out_shape = (shape(size, slots),) * (len(turns) + 1) if turns else (shape(sizes[1], size, slots),)
     flat = lambda kind, *dims: jax.ShapeDtypeStruct(dims, kind)
@@ -524,7 +530,7 @@
         name="forces",
     )(rows, *found, got_c, got_d)
     if turns:
-        arrived = [swap(value, round_pairs(sizes, turn)) for value, turn in zip(sent, turns)]
+        arrived = [lax.ppermute(value, "gy", list(enumerate(turn))) for value, turn in zip(sent, turns)]
         arrived.append(sent[-1])
         scratch = [pltpu.VMEM((sizes[1], size, slots), jnp.float32)]
     else:

time: 20.4 us -> 20 us (0.980)
  waiting for transfers between devices: 6.52 us -> 6.28 us
    ppermute x7 -> x4, starting transfers between devices: 10.5 us -> 5.21 us  [swap(): return lax.ppermute(value, ('gx', 'gy'), pairs)]
    ppermute x0 -> x3, starting transfers between devices: none -> 5.04 us  [per_device(): lax.ppermute(value, 'gy', list(enumerate(turn)))]
    ppermute x7 -> x4, waiting for transfers between devices: 6.52 us -> 3.04 us  [swap(): return lax.ppermute(value, ('gx', 'gy'), pairs)]
    ppermute x0 -> x3, waiting for transfers between devices: none -> 3.24 us  [per_device(): lax.ppermute(value, 'gy', list(enumerate(turn)))]
  transfers between devices with their start and end apart: 7 -> 7, of which waited for: 4 -> 5; matrix products, arithmetic and copies ran while one was open for 0% -> 0% of each run, Pallas kernels for 2% -> 2%
where the time goes in v6:
time: 20 us; the launch traced here: 19.7 us
  starting transfers between devices  10.3 us (52%)
  waiting for transfers between devices  6.28 us (31%)
  Pallas kernels  3.14 us (16%)
    ppermute x4, starting transfers between devices, swap(): return lax.ppermute(value, ('gx', 'gy'), pairs)  5.21 us
    ppermute x3, starting transfers between devices, per_device(): lax.ppermute(value, 'gy', list(enumerate(turn)))  5.04 us
    ppermute x3, waiting for transfers between devices, per_device(): lax.ppermute(value, 'gy', list(enumerate(turn)))  3.24 us
    ppermute x4, waiting for transfers between devices, swap(): return lax.ppermute(value, ('gx', 'gy'), pairs)  3.04 us
    pallas_call x1, Pallas kernels, per_device(): pl.pallas_call(functools.partial(force_kernel, counts=sizes, cells_x=cell...  1.22 us
    pallas_call x1, Pallas kernels, per_device(): pl.pallas_call(functools.partial(prepare_kernel, capacity=capacity), out_...  0.9 us
    pallas_call x1, Pallas kernels, per_device(): pl.pallas_call(functools.partial(gather_kernel, count=sizes[1], cells_x=c...  0.64 us
  transfers between devices with their start and end apart: 7, of which 5 were waited for; matrix products, arithmetic and copies ran while one was open for 0% of the time, Pallas kernels for 2%

profile of v6, /device:TPU:0, one launch (start us, length us, event | category | flops | bytes accessed | tf_op | source)
XLA Modules:
  0.0 19.7 jit_solution(4327252375710261824)
XLA Ops:
  0.0 0.9 %prepare.1 = (f32[32,128]{1,0:T(8,128)S(1)}, f32[32,128]{1,0:T(8,128)S(1)}, f32[32,128]{1,0:T(8,128)S(1)}) custom-call(f32[3,2,2,128]{3,2,1,0:T(2,128)} %disp_in.1, f32[3,2,2,128]{3,2,1,0:T(2,128)} %vel_in.1, f32[3,2,2,128]{3,2,1,0:T(2,128)} %force_in.1, s32[2,2,128]{2,1,0:T(2,128)} %heights_in.1, s32[2,2]{1,0:T(2,128)} %counts_in.1, ...), custom_call_target="tpu_custom_call" | custom-call | tf_op jit(solution)/shard_map/prepare/pallas_call | solution.py:466
  0.9 3.1 %collective-permute-start.1 = (f32[32,128]{1,0:T(8,128)S(1)}, f32[32,128]{1,0:T(8,128)S(1)}, u32[]{:S(2)}, u32[]{:S(2)}) collective-permute-start(f32[32,128]{1,0:T(8,128)S(1)} %get-tuple-element.23), channel_id=1, source_target_pairs={{0,1},{1,0},{2,3},{3,2},{4,8},{5,9},{6,10},{7,11},{8,4},{9,5},{10,... | collective-permute-start | bytes 49160 | tf_op jit(solution)/shard_map/ppermute | solution.py:463
  4.0 0.0 copy-start
  4.0 0.0 collective-permute-start
  4.1 1.7 %collective-permute-done.1.got_b = f32[32,128]{1,0:T(8,128)S(1)} collective-permute-done((f32[32,128]{1,0:T(8,128)S(1)}, f32[32,128]{1,0:T(8,128)S(1)}, u32[]{:S(2)}, u32[]{:S(2)}) %collective-permute-start.1) | collective-permute-done | bytes 16416 | tf_op jit(solution)/shard_map/ppermute | solution.py:463
  5.7 0.0 collective-permute-done.got_a
  5.8 0.0 collective-permute-start.2
  5.8 2.0 %collective-permute-start.3 = (f32[24,128]{1,0:T(8,128)S(1)}, f32[24,128]{1,0:T(8,128)S(1)}, u32[]{:S(2)}, u32[]{:S(2)}) collective-permute-start(f32[24,128]{1,0:T(8,128)S(1)} %get-tuple-element.32), channel_id=1, source_target_pairs={{0,1},{1,2},{2,3},{3,7},{4,0},{5,4},{6,5},{7,6},{8,9},{9,10},{10,1... | collective-permute-start | bytes 36872 | tf_op jit(solution)/shard_map/ppermute | solution.py:463
  7.8 0.0 copy-done
  7.8 0.4 %near.1 = (f32[4,8,128]{2,1,0:T(8,128)S(1)}, f32[8,3,8,128]{3,2,1,0:T(8,128)S(1)}, s32[8,8,128]{2,1,0:T(8,128)S(1)}, s32[8,8,128]{2,1,0:T(8,128)S(1)}, f32[64,128]{1,0:T(8,128)S(1)}, /*index=5*/f32[64,128]{1,0:T(8,128)S(1)}) custom-call(f32[4,2,6,128]{3,2,1,0:T(8,128)S(1)} %get-tuple-element.24.middle, f32[32,128]{1,0:T(8,128)S(1)} %collective-permute-done.got_a, ...), custom_call_target="tpu_custom_call" | custom-call | flops 1000000 | bytes 200000 | tf_op jit(solution)/shard_map/near/pallas_call | solution.py:498
  8.2 1.3 %collective-permute-done.2.got_c = f32[24,128]{1,0:T(8,128)S(1)} collective-permute-done((f32[24,128]{1,0:T(8,128)S(1)}, f32[24,128]{1,0:T(8,128)S(1)}, u32[]{:S(2)}, u32[]{:S(2)}) %collective-permute-start.2) | collective-permute-done | bytes 12320 | tf_op jit(solution)/shard_map/ppermute | solution.py:463
  9.6 0.0 collective-permute-done.3.got_d
  9.6 1.2 %forces.1 = (f32[28,128]{1,0:T(8,128)S(1)}, f32[28,128]{1,0:T(8,128)S(1)}, f32[28,128]{1,0:T(8,128)S(1)}, f32[28,128]{1,0:T(8,128)S(1)}) custom-call(f32[32,128]{1,0:T(8,128)S(1)} %get-tuple-element.21.rows, f32[4,8,128]{2,1,0:T(8,128)S(1)} %get-tuple-element.25.centre, f32[8,3,8,128]{3,2,1,0:T(8,128)S(1)} %get-tuple-element.26.nearby_own, ...), custom_call_target="tpu_custom_call" | custom-call | tf_op jit(solution)/shard_map/forces/pallas_call | solution.py:518
  10.8 3.5 %collective-permute-start.4 = (f32[28,128]{1,0:T(8,128)S(1)}, f32[28,128]{1,0:T(8,128)S(1)}, u32[]{:S(2)}, u32[]{:S(2)}) collective-permute-start(f32[28,128]{1,0:T(8,128)S(1)} %get-tuple-element.33), channel_id=1, source_target_pairs={{0,2},{1,3},{2,1},{3,0},{4,6},{5,7},{6,5},{7,4},{8,10},{9,11},{10,... | collective-permute-start | bytes 43016 | tf_op jit(solution)/shard_map/ppermute | solution.py:533
  14.3 1.1 %collective-permute-start.5 = (f32[28,128]{1,0:T(8,128)S(1)}, f32[28,128]{1,0:T(8,128)S(1)}, u32[]{:S(2)}, u32[]{:S(2)}) collective-permute-start(f32[28,128]{1,0:T(8,128)S(1)} %get-tuple-element.34), channel_id=1, source_target_pairs={{0,3},{1,2},{2,0},{3,1},{4,7},{5,6},{6,4},{7,5},{8,11},{9,10},{10,... | collective-permute-start | bytes 43016 | tf_op jit(solution)/shard_map/ppermute | solution.py:533
  15.3 0.5 %collective-permute-start.6 = (f32[28,128]{1,0:T(8,128)S(1)}, f32[28,128]{1,0:T(8,128)S(1)}, u32[]{:S(2)}, u32[]{:S(2)}) collective-permute-start(f32[28,128]{1,0:T(8,128)S(1)} %get-tuple-element.35), channel_id=1, source_target_pairs={{0,1},{1,0},{2,3},{3,2},{4,5},{5,4},{6,7},{7,6},{8,9},{9,8},{10,11... | collective-permute-start | bytes 43016 | tf_op jit(solution)/shard_map/ppermute | solution.py:533
  15.8 1.2 %collective-permute-done.4.refs_0_ = f32[28,128]{1,0:T(8,128)S(1)} collective-permute-done((f32[28,128]{1,0:T(8,128)S(1)}, f32[28,128]{1,0:T(8,128)S(1)}, u32[]{:S(2)}, u32[]{:S(2)}) %collective-permute-start.4) | collective-permute-done | bytes 14368 | tf_op jit(solution)/shard_map/ppermute | solution.py:533
  17.0 1.9 %collective-permute-done.5.refs_1_ = f32[28,128]{1,0:T(8,128)S(1)} collective-permute-done((f32[28,128]{1,0:T(8,128)S(1)}, f32[28,128]{1,0:T(8,128)S(1)}, u32[]{:S(2)}, u32[]{:S(2)}) %collective-permute-start.5) | collective-permute-done | bytes 14368 | tf_op jit(solution)/shard_map/ppermute | solution.py:533
  18.9 0.2 collective-permute-done.6.refs_2_
  19.1 0.6 %collect.1 = f32[4,7,2,128]{3,2,1,0:T(2,128)} custom-call(f32[28,128]{1,0:T(8,128)S(1)} %collective-permute-done.4.refs_0_, f32[28,128]{1,0:T(8,128)S(1)} %collective-permute-done.5.refs_1_, f32[28,128]{1,0:T(8,128)S(1)} %collective-permute-done.6.refs_2_, f32[28,128]{1,0:T(8,128)S(1)} %get-tuple-element.36.refs_3_), custom_call_target="tpu_custom_call" | custom-call | tf_op jit(solution)/shard_map/collect/pallas_call | solution.py:539
  (1 shorter events, 0.0 us)
Async XLA Ops:
  0.9 4.8 %collective-permute-start.1 = (f32[32,128]{1,0:T(8,128)S(1)}, f32[32,128]{1,0:T(8,128)S(1)}, u32[]{:S(2)}, u32[]{:S(2)}) collective-permute-start(f32[32,128]{1,0:T(8,128)S(1)} %get-tuple-element.23), channel_id=1, source_target_pairs={{0,1},{1,0},{2,3},{3,2},{4,8},{5,9},{6,10},{7,11},{8,4},{9,5},{10,... | collective-permute-start | bytes 49160 | tf_op jit(solution)/shard_map/ppermute | solution.py:463
  4.0 3.8 %copy-start = (s32[8,2,2,128]{3,2,1,0:T(2,128)S(1)}, s32[8,2,2,128]{3,2,1,0:T(2,128)}, u32[]{:S(2)}) copy-start(s32[8,2,2,128]{3,2,1,0:T(2,128)} %lists.1) | copy-start | bytes 49156
  4.0 1.7 %collective-permute-start = (f32[32,128]{1,0:T(8,128)S(1)}, f32[32,128]{1,0:T(8,128)S(1)}, u32[]{:S(2)}, u32[]{:S(2)}) collective-permute-start(f32[32,128]{1,0:T(8,128)S(1)} %get-tuple-element.22.own), channel_id=1, source_target_pairs={{0,4},{1,5},{2,6},{3,7},{4,0},{5,1},{6,2},{7,3},{8,12},{9,13},{10,... | collective-permute-start | bytes 49160 | tf_op jit(solution)/shard_map/ppermute | solution.py:463
  5.8 3.8 %collective-permute-start.2 = (f32[24,128]{1,0:T(8,128)S(1)}, f32[24,128]{1,0:T(8,128)S(1)}, u32[]{:S(2)}, u32[]{:S(2)}) collective-permute-start(f32[24,128]{1,0:T(8,128)S(1)} %get-tuple-element.31), channel_id=1, source_target_pairs={{0,4},{1,0},{2,1},{3,2},{4,5},{5,6},{6,7},{7,3},{8,12},{9,8},{10,9... | collective-permute-start | bytes 36872 | tf_op jit(solution)/shard_map/ppermute | solution.py:463
  5.8 3.7 %collective-permute-start.3 = (f32[24,128]{1,0:T(8,128)S(1)}, f32[24,128]{1,0:T(8,128)S(1)}, u32[]{:S(2)}, u32[]{:S(2)}) collective-permute-start(f32[24,128]{1,0:T(8,128)S(1)} %get-tuple-element.32), channel_id=1, source_target_pairs={{0,1},{1,2},{2,3},{3,7},{4,0},{5,4},{6,5},{7,6},{8,9},{9,10},{10,1... | collective-permute-start | bytes 36872 | tf_op jit(solution)/shard_map/ppermute | solution.py:463
  10.8 6.2 %collective-permute-start.4 = (f32[28,128]{1,0:T(8,128)S(1)}, f32[28,128]{1,0:T(8,128)S(1)}, u32[]{:S(2)}, u32[]{:S(2)}) collective-permute-start(f32[28,128]{1,0:T(8,128)S(1)} %get-tuple-element.33), channel_id=1, source_target_pairs={{0,2},{1,3},{2,1},{3,0},{4,6},{5,7},{6,5},{7,4},{8,10},{9,11},{10,... | collective-permute-start | bytes 43016 | tf_op jit(solution)/shard_map/ppermute | solution.py:533
  14.3 4.6 %collective-permute-start.5 = (f32[28,128]{1,0:T(8,128)S(1)}, f32[28,128]{1,0:T(8,128)S(1)}, u32[]{:S(2)}, u32[]{:S(2)}) collective-permute-start(f32[28,128]{1,0:T(8,128)S(1)} %get-tuple-element.34), channel_id=1, source_target_pairs={{0,3},{1,2},{2,0},{3,1},{4,7},{5,6},{6,4},{7,5},{8,11},{9,10},{10,... | collective-permute-start | bytes 43016 | tf_op jit(solution)/shard_map/ppermute | solution.py:533
  15.3 3.7 %collective-permute-start.6 = (f32[28,128]{1,0:T(8,128)S(1)}, f32[28,128]{1,0:T(8,128)S(1)}, u32[]{:S(2)}, u32[]{:S(2)}) collective-permute-start(f32[28,128]{1,0:T(8,128)S(1)} %get-tuple-element.35), channel_id=1, source_target_pairs={{0,1},{1,0},{2,3},{3,2},{4,5},{5,4},{6,7},{7,6},{8,9},{9,8},{10,11... | collective-permute-start | bytes 43016 | tf_op jit(solution)/shard_map/ppermute | solution.py:533

commit v7 on v6

--- a/solution.py
+++ b/solution.py
@@ -156,7 +156,7 @@
 
 
 def half_wave(radius):
-    angle = half_pi * (jnp.clip(radius, 2.7, 3.0) - 2.85) / 0.15
+    angle = (jnp.clip(radius, 2.7, 3.0) - 2.85) * (half_pi / 0.15)
     square = angle * angle
     sine, cosine = 0.0, 0.0
     for odd in (15, 13, 11, 9, 7, 5, 3, 1):
@@ -442,9 +442,8 @@
                     if 0 <= other < count:
                         part = held[other, pl.ds(first + (2 * x + side) * 3, 3), :]
                         speed = speed + jnp.where(name == float(x * cells_y + y + 1), part, 0.0)
-            for line in range(7):
-                value = speed[line - 3 : line - 2] if 3 <= line < 6 else block[line : line + 1]
-                out[source, line, pl.ds(slot, 1), :] = value
+            lines = pl.ds(source * 7 * capacity + slot, 7, stride=capacity)
+            out[lines, :] = jnp.concatenate([block[:3], speed, block[6:7]], axis=0)
 
 
 def per_device(displacement, velocity, forces, heights, counts, neighbours, plan):
@@ -540,14 +539,14 @@
         functools.partial(
             gather_kernel, count=sizes[1], cells_x=cells_x, cells_y=cells_y, capacity=capacity, turns=turns
         ),
-        out_shape=shape(sizes[1], 7, capacity, slots),
+        out_shape=shape(sizes[1] * 7 * capacity, slots),
         in_specs=[whole] * len(arrived),
         out_specs=whole,
         scratch_shapes=scratch,
         compiler_params=pltpu.CompilerParams(vmem_limit_bytes=VMEM_BYTES),
         name="collect",
     )(*arrived)
-    return jnp.swapaxes(result, 1, 2)[None, None]
+    return jnp.swapaxes(result.reshape(sizes[1], 7, capacity, slots), 1, 2)[None, None]
 
 
 def solution(mesh):

time: 20 us -> 20 us (level)
  no operation moved by 1% of the time
where the time goes in v7:
time: 20 us; the launch traced here: 19.7 us
  starting transfers between devices  10.3 us (52%)
  waiting for transfers between devices  6.28 us (31%)
  Pallas kernels  3.14 us (16%)
    ppermute x4, starting transfers between devices, swap(): return lax.ppermute(value, ('gx', 'gy'), pairs)  5.21 us
    ppermute x3, starting transfers between devices, per_device(): lax.ppermute(value, 'gy', list(enumerate(turn)))  5.04 us
    ppermute x3, waiting for transfers between devices, per_device(): lax.ppermute(value, 'gy', list(enumerate(turn)))  3.24 us
    ppermute x4, waiting for transfers between devices, swap(): return lax.ppermute(value, ('gx', 'gy'), pairs)  3.04 us
    pallas_call x1, Pallas kernels, per_device(): pl.pallas_call(functools.partial(force_kernel, counts=sizes, cells_x=cell...  1.22 us
    pallas_call x1, Pallas kernels, per_device(): pl.pallas_call(functools.partial(prepare_kernel, capacity=capacity), out_...  0.9 us
    pallas_call x1, Pallas kernels, per_device(): pl.pallas_call(functools.partial(gather_kernel, count=sizes[1], cells_x=c...  0.64 us
  transfers between devices with their start and end apart: 7, of which 5 were waited for; matrix products, arithmetic and copies ran while one was open for 0% of the time, Pallas kernels for 2%

profile of v7, /device:TPU:0, one launch (start us, length us, event | category | flops | bytes accessed | tf_op | source)
XLA Modules:
  0.0 19.7 jit_solution(17078545489495251045)
XLA Ops:
  0.0 0.9 %prepare.1 = (f32[32,128]{1,0:T(8,128)S(1)}, f32[32,128]{1,0:T(8,128)S(1)}, f32[32,128]{1,0:T(8,128)S(1)}) custom-call(f32[3,2,2,128]{3,2,1,0:T(2,128)} %disp_in.1, f32[3,2,2,128]{3,2,1,0:T(2,128)} %vel_in.1, f32[3,2,2,128]{3,2,1,0:T(2,128)} %force_in.1, s32[2,2,128]{2,1,0:T(2,128)} %heights_in.1, s32[2,2]{1,0:T(2,128)} %counts_in.1, ...), custom_call_target="tpu_custom_call" | custom-call | tf_op jit(solution)/shard_map/prepare/pallas_call | solution.py:465
  0.9 3.1 %collective-permute-start.1 = (f32[32,128]{1,0:T(8,128)S(1)}, f32[32,128]{1,0:T(8,128)S(1)}, u32[]{:S(2)}, u32[]{:S(2)}) collective-permute-start(f32[32,128]{1,0:T(8,128)S(1)} %get-tuple-element.23), channel_id=1, source_target_pairs={{0,1},{1,0},{2,3},{3,2},{4,8},{5,9},{6,10},{7,11},{8,4},{9,5},{10,... | collective-permute-start | bytes 49160 | tf_op jit(solution)/shard_map/ppermute | solution.py:462
  4.0 0.0 copy-start
  4.0 0.0 collective-permute-start
  4.1 1.7 %collective-permute-done.1.got_b = f32[32,128]{1,0:T(8,128)S(1)} collective-permute-done((f32[32,128]{1,0:T(8,128)S(1)}, f32[32,128]{1,0:T(8,128)S(1)}, u32[]{:S(2)}, u32[]{:S(2)}) %collective-permute-start.1) | collective-permute-done | bytes 16416 | tf_op jit(solution)/shard_map/ppermute | solution.py:462
  5.7 0.0 collective-permute-done.got_a
  5.8 0.0 collective-permute-start.2
  5.8 2.0 %collective-permute-start.3 = (f32[24,128]{1,0:T(8,128)S(1)}, f32[24,128]{1,0:T(8,128)S(1)}, u32[]{:S(2)}, u32[]{:S(2)}) collective-permute-start(f32[24,128]{1,0:T(8,128)S(1)} %get-tuple-element.32), channel_id=1, source_target_pairs={{0,1},{1,2},{2,3},{3,7},{4,0},{5,4},{6,5},{7,6},{8,9},{9,10},{10,1... | collective-permute-start | bytes 36872 | tf_op jit(solution)/shard_map/ppermute | solution.py:462
  7.8 0.0 copy-done
  7.8 0.4 %near.1 = (f32[4,8,128]{2,1,0:T(8,128)S(1)}, f32[8,3,8,128]{3,2,1,0:T(8,128)S(1)}, s32[8,8,128]{2,1,0:T(8,128)S(1)}, s32[8,8,128]{2,1,0:T(8,128)S(1)}, f32[64,128]{1,0:T(8,128)S(1)}, /*index=5*/f32[64,128]{1,0:T(8,128)S(1)}) custom-call(f32[4,2,6,128]{3,2,1,0:T(8,128)S(1)} %get-tuple-element.24.middle, f32[32,128]{1,0:T(8,128)S(1)} %collective-permute-done.got_a, ...), custom_call_target="tpu_custom_call" | custom-call | flops 1000000 | bytes 200000 | tf_op jit(solution)/shard_map/near/pallas_call | solution.py:497
  8.2 1.3 %collective-permute-done.2.got_c = f32[24,128]{1,0:T(8,128)S(1)} collective-permute-done((f32[24,128]{1,0:T(8,128)S(1)}, f32[24,128]{1,0:T(8,128)S(1)}, u32[]{:S(2)}, u32[]{:S(2)}) %collective-permute-start.2) | collective-permute-done | bytes 12320 | tf_op jit(solution)/shard_map/ppermute | solution.py:462
  9.6 0.0 collective-permute-done.3.got_d
  9.6 1.2 %forces.1 = (f32[28,128]{1,0:T(8,128)S(1)}, f32[28,128]{1,0:T(8,128)S(1)}, f32[28,128]{1,0:T(8,128)S(1)}, f32[28,128]{1,0:T(8,128)S(1)}) custom-call(f32[32,128]{1,0:T(8,128)S(1)} %get-tuple-element.21.rows, f32[4,8,128]{2,1,0:T(8,128)S(1)} %get-tuple-element.25.centre, f32[8,3,8,128]{3,2,1,0:T(8,128)S(1)} %get-tuple-element.26.nearby_own, ...), custom_call_target="tpu_custom_call" | custom-call | tf_op jit(solution)/shard_map/forces/pallas_call | solution.py:517
  10.8 3.5 %collective-permute-start.4 = (f32[28,128]{1,0:T(8,128)S(1)}, f32[28,128]{1,0:T(8,128)S(1)}, u32[]{:S(2)}, u32[]{:S(2)}) collective-permute-start(f32[28,128]{1,0:T(8,128)S(1)} %get-tuple-element.33), channel_id=1, source_target_pairs={{0,2},{1,3},{2,1},{3,0},{4,6},{5,7},{6,5},{7,4},{8,10},{9,11},{10,... | collective-permute-start | bytes 43016 | tf_op jit(solution)/shard_map/ppermute | solution.py:532
  14.2 1.1 %collective-permute-start.5 = (f32[28,128]{1,0:T(8,128)S(1)}, f32[28,128]{1,0:T(8,128)S(1)}, u32[]{:S(2)}, u32[]{:S(2)}) collective-permute-start(f32[28,128]{1,0:T(8,128)S(1)} %get-tuple-element.34), channel_id=1, source_target_pairs={{0,3},{1,2},{2,0},{3,1},{4,7},{5,6},{6,4},{7,5},{8,11},{9,10},{10,... | collective-permute-start | bytes 43016 | tf_op jit(solution)/shard_map/ppermute | solution.py:532
  15.3 0.5 %collective-permute-start.6 = (f32[28,128]{1,0:T(8,128)S(1)}, f32[28,128]{1,0:T(8,128)S(1)}, u32[]{:S(2)}, u32[]{:S(2)}) collective-permute-start(f32[28,128]{1,0:T(8,128)S(1)} %get-tuple-element.35), channel_id=1, source_target_pairs={{0,1},{1,0},{2,3},{3,2},{4,5},{5,4},{6,7},{7,6},{8,9},{9,8},{10,11... | collective-permute-start | bytes 43016 | tf_op jit(solution)/shard_map/ppermute | solution.py:532
  15.8 1.3 %collective-permute-done.4.refs_0_ = f32[28,128]{1,0:T(8,128)S(1)} collective-permute-done((f32[28,128]{1,0:T(8,128)S(1)}, f32[28,128]{1,0:T(8,128)S(1)}, u32[]{:S(2)}, u32[]{:S(2)}) %collective-permute-start.4) | collective-permute-done | bytes 14368 | tf_op jit(solution)/shard_map/ppermute | solution.py:532
  17.1 1.8 %collective-permute-done.5.refs_1_ = f32[28,128]{1,0:T(8,128)S(1)} collective-permute-done((f32[28,128]{1,0:T(8,128)S(1)}, f32[28,128]{1,0:T(8,128)S(1)}, u32[]{:S(2)}, u32[]{:S(2)}) %collective-permute-start.5) | collective-permute-done | bytes 14368 | tf_op jit(solution)/shard_map/ppermute | solution.py:532
  18.9 0.2 collective-permute-done.6.refs_2_
  19.1 0.6 %collect.1 = f32[56,128]{1,0:T(8,128)} custom-call(f32[28,128]{1,0:T(8,128)S(1)} %collective-permute-done.4.refs_0_, f32[28,128]{1,0:T(8,128)S(1)} %collective-permute-done.5.refs_1_, f32[28,128]{1,0:T(8,128)S(1)} %collective-permute-done.6.refs_2_, f32[28,128]{1,0:T(8,128)S(1)} %get-tuple-element.36.refs_3_), custom_call_target="tpu_custom_call" | custom-call | tf_op jit(solution)/shard_map/collect/pallas_call | solution.py:538
  (1 shorter events, 0.0 us)
Async XLA Ops:
  0.9 4.8 %collective-permute-start.1 = (f32[32,128]{1,0:T(8,128)S(1)}, f32[32,128]{1,0:T(8,128)S(1)}, u32[]{:S(2)}, u32[]{:S(2)}) collective-permute-start(f32[32,128]{1,0:T(8,128)S(1)} %get-tuple-element.23), channel_id=1, source_target_pairs={{0,1},{1,0},{2,3},{3,2},{4,8},{5,9},{6,10},{7,11},{8,4},{9,5},{10,... | collective-permute-start | bytes 49160 | tf_op jit(solution)/shard_map/ppermute | solution.py:462
  4.0 3.8 %copy-start = (s32[8,2,2,128]{3,2,1,0:T(2,128)S(1)}, s32[8,2,2,128]{3,2,1,0:T(2,128)}, u32[]{:S(2)}) copy-start(s32[8,2,2,128]{3,2,1,0:T(2,128)} %lists.1) | copy-start | bytes 49156
  4.0 1.7 %collective-permute-start = (f32[32,128]{1,0:T(8,128)S(1)}, f32[32,128]{1,0:T(8,128)S(1)}, u32[]{:S(2)}, u32[]{:S(2)}) collective-permute-start(f32[32,128]{1,0:T(8,128)S(1)} %get-tuple-element.22.own), channel_id=1, source_target_pairs={{0,4},{1,5},{2,6},{3,7},{4,0},{5,1},{6,2},{7,3},{8,12},{9,13},{10,... | collective-permute-start | bytes 49160 | tf_op jit(solution)/shard_map/ppermute | solution.py:462
  5.8 3.8 %collective-permute-start.2 = (f32[24,128]{1,0:T(8,128)S(1)}, f32[24,128]{1,0:T(8,128)S(1)}, u32[]{:S(2)}, u32[]{:S(2)}) collective-permute-start(f32[24,128]{1,0:T(8,128)S(1)} %get-tuple-element.31), channel_id=1, source_target_pairs={{0,4},{1,0},{2,1},{3,2},{4,5},{5,6},{6,7},{7,3},{8,12},{9,8},{10,9... | collective-permute-start | bytes 36872 | tf_op jit(solution)/shard_map/ppermute | solution.py:462
  5.8 3.7 %collective-permute-start.3 = (f32[24,128]{1,0:T(8,128)S(1)}, f32[24,128]{1,0:T(8,128)S(1)}, u32[]{:S(2)}, u32[]{:S(2)}) collective-permute-start(f32[24,128]{1,0:T(8,128)S(1)} %get-tuple-element.32), channel_id=1, source_target_pairs={{0,1},{1,2},{2,3},{3,7},{4,0},{5,4},{6,5},{7,6},{8,9},{9,10},{10,1... | collective-permute-start | bytes 36872 | tf_op jit(solution)/shard_map/ppermute | solution.py:462
  10.8 6.3 %collective-permute-start.4 = (f32[28,128]{1,0:T(8,128)S(1)}, f32[28,128]{1,0:T(8,128)S(1)}, u32[]{:S(2)}, u32[]{:S(2)}) collective-permute-start(f32[28,128]{1,0:T(8,128)S(1)} %get-tuple-element.33), channel_id=1, source_target_pairs={{0,2},{1,3},{2,1},{3,0},{4,6},{5,7},{6,5},{7,4},{8,10},{9,11},{10,... | collective-permute-start | bytes 43016 | tf_op jit(solution)/shard_map/ppermute | solution.py:532
  14.2 4.6 %collective-permute-start.5 = (f32[28,128]{1,0:T(8,128)S(1)}, f32[28,128]{1,0:T(8,128)S(1)}, u32[]{:S(2)}, u32[]{:S(2)}) collective-permute-start(f32[28,128]{1,0:T(8,128)S(1)} %get-tuple-element.34), channel_id=1, source_target_pairs={{0,3},{1,2},{2,0},{3,1},{4,7},{5,6},{6,4},{7,5},{8,11},{9,10},{10,... | collective-permute-start | bytes 43016 | tf_op jit(solution)/shard_map/ppermute | solution.py:532
  15.3 3.7 %collective-permute-start.6 = (f32[28,128]{1,0:T(8,128)S(1)}, f32[28,128]{1,0:T(8,128)S(1)}, u32[]{:S(2)}, u32[]{:S(2)}) collective-permute-start(f32[28,128]{1,0:T(8,128)S(1)} %get-tuple-element.35), channel_id=1, source_target_pairs={{0,1},{1,0},{2,3},{3,2},{4,5},{5,4},{6,7},{7,6},{8,9},{9,8},{10,11... | collective-permute-start | bytes 43016 | tf_op jit(solution)/shard_map/ppermute | solution.py:532
